TPU v7x, 32 devices: a whole 2x2x4 slice. The times are simulated.
32 devices in a mesh: member: 4 (over x, core), space: 8 (over z, y).
Axes of the slice: x: 2, y: 2, z: 4, core: 2. Of those that a mesh axis runs over, the one named last changes fastest.
Arguments:
- members: float32 [16, 16, 2, 368, 384], P('member', None, None, 'space'), may hold values from -6 to 6
- target: float32 [16, 2, 368, 384], P('member', None, 'space'), may hold values from -6 to 6
- order_table: int32 [368], replicated, may hold values from 0 to 367, each once
Outputs:
- field_grad: float32 [16, 16, 368, 720], P('member', None, 'space')
Inputs may be any that keep to these rules, and one draw needn't show every extreme that they name: Slot p of the order dimension of members and target holds order order_table[p]; each of 0 to 367 appears once, and orders above 360 are empty slots.
All inputs are finite; a program needn't handle non-finite values.
Results may differ from a plain program's by a relative error of at most 0.0003.
Values sent between devices are 32-bit elements; how exact they have to be, the bound alone decides.
No kernel may reach another device: no remote copies, remote signals or barrier semaphores. Data moves between devices by JAX's collectives and lax.ppermute only.
A program may use at most 192 MiB of HBM per device.

v0:
```python
import math

import jax
import jax.numpy as jnp
from jax import lax
from jax.sharding import PartitionSpec as P

LMAX = 360
NLAT = 361
NLON = 720


smooth_eps = 0.01
log_gamma_half = 0.5 * math.log(math.pi) - math.log(2.0)


def legendre_table(orders, lmax, nlat, lpad, nlatp):
    rows = jnp.arange(nlatp, dtype=jnp.int32)
    row_f = rows.astype(jnp.float32)
    span = float(nlat - 1)
    theta = jnp.pi * row_f / span
    nearest = jnp.clip(jnp.minimum(row_f, span - row_f), 0.0, None)
    sines = jnp.sin(jnp.pi * nearest / span)
    cosines = jnp.cos(theta)
    lat_weight = jnp.where(rows < nlat, sines, 0.0)
    order_i = jnp.minimum(orders, lmax)
    order_f = order_i.astype(jnp.float32)
    log_base = 0.5 * (
        math.log(1.0 / (4.0 * math.pi))
        + lax.lgamma(order_f + 1.5)
        - log_gamma_half
        - lax.lgamma(order_f + 1.0)
    )
    order_col = order_i[:, None]
    order_fc = order_f[:, None]
    log_sine = jnp.log(jnp.where(sines > 0.0, sines, 1.0))
    polar_zero = (sines[None, :] <= 0.0) & (order_fc > 0.0)
    start_value = jnp.where(polar_zero, 0.0, 1.0)
    start_scale = jnp.where(polar_zero, 0.0, log_base[:, None] + order_fc * log_sine[None, :])

    def step(carry, degree):
        prev, prev2, scale = carry
        deg_f = degree.astype(jnp.float32)
        coef_a = jnp.sqrt(
            jnp.maximum(4.0 * deg_f * deg_f - 1.0, 1.0)
            / jnp.maximum(deg_f * deg_f - order_fc * order_fc, 1.0)
        )
        lower = deg_f - 1.0
        coef_b = jnp.sqrt(
            jnp.maximum(lower * lower - order_fc * order_fc, 0.0)
            / jnp.maximum(4.0 * lower * lower - 1.0, 1.0)
        )
        recur = coef_a * (cosines[None, :] * prev - coef_b * prev2)
        at_start = degree == order_col
        current = jnp.where(degree < order_col, 0.0, jnp.where(at_start, start_value, recur))
        scale_now = jnp.where(at_start, start_scale, scale)
        shifted = jnp.where(at_start, 0.0, prev)
        largest = jnp.maximum(jnp.abs(current), jnp.abs(shifted))
        divisor = jnp.where(largest > 0.0, largest, 1.0)
        current_n = current / divisor
        shifted_n = shifted / divisor
        scale_n = scale_now + jnp.log(divisor)
        return ((current_n, shifted_n, scale_n), current_n * jnp.exp(scale_n))

    zeros = jnp.zeros((orders.shape[0], nlatp), jnp.float32)
    _, stacked = lax.scan(step, (zeros, zeros, zeros), jnp.arange(lpad, dtype=jnp.int32), unroll=16)
    table = jnp.transpose(stacked, (1, 0, 2))
    degrees = jnp.arange(lpad, dtype=jnp.int32)
    valid = (degrees[None, :] <= lmax) & (orders[:, None] <= lmax)
    return jnp.where(valid[:, :, None], table, 0.0) * lat_weight[None, None, :]


def loss_weight(orders, lmax, lpad):
    degrees = jnp.arange(lpad, dtype=jnp.int32)[None, :]
    order_col = orders[:, None]
    valid = (degrees >= order_col) & (degrees <= lmax) & (order_col <= lmax)
    doubled = jnp.where(order_col == 0, 1.0, 2.0)
    return jnp.where(valid, doubled, 0.0).astype(jnp.float32)


def pair_gradient(rows, ensemble, targets, orders, lmax):
    count = ensemble.shape[0]
    weight = loss_weight(orders, lmax, ensemble.shape[4])
    diff = rows - targets[None]
    size = jnp.sqrt(jnp.sum(diff * diff, axis=2, keepdims=True) + smooth_eps)

    def against(single):
        delta = single[None] - ensemble
        dist = jnp.sqrt(jnp.sum(delta * delta, axis=2, keepdims=True) + smooth_eps)
        return jnp.sum(delta / dist, axis=0)

    spread = lax.map(against, rows)
    return (diff / size / count - spread / (count * (count - 1))) * weight


def to_latitudes(grads, table):
    return jnp.einsum("ecrml,mlj->ecjrm", grads, table, precision=lax.Precision.HIGHEST)


def longitude_basis(orders, nlon, lmax):
    cols = jnp.arange(nlon, dtype=jnp.int32)
    phase = orders[:, None] * cols[None, :] % nlon
    angle = 2.0 * jnp.pi * phase.astype(jnp.float32) / nlon
    valid = (orders <= lmax)[:, None]
    scale = 2.0 * jnp.pi / nlon
    cosine = jnp.where(valid, jnp.cos(angle), 0.0) * scale
    sine = jnp.where(valid, -jnp.sin(angle), 0.0) * scale
    return jnp.stack([cosine, sine], axis=0)


def to_longitudes(lat_grad, basis):
    ens, chans, lats, parts, slots = lat_grad.shape
    flat = lat_grad.reshape(ens * chans * lats, parts * slots)
    result = jnp.dot(
        flat,
        basis.reshape(parts * slots, basis.shape[2]),
        precision=lax.Precision.HIGHEST,
        preferred_element_type=jnp.float32,
    )
    return result.reshape(ens, chans, lats, basis.shape[2])


def shards(members, target, order_table):
    slots_dev = members.shape[3]
    deg_slots = members.shape[4]
    space_count = lax.axis_size("space")
    nlat_pad = (NLAT + space_count - 1) // space_count * space_count
    my_orders = lax.dynamic_slice_in_dim(
        order_table, lax.axis_index("space") * slots_dev, slots_dev
    )
    table = legendre_table(my_orders, LMAX, NLAT, deg_slots, nlat_pad)
    basis = longitude_basis(order_table, NLON, LMAX)
    everyone, all_targets = (
        lax.all_gather(members, "member", axis=0, tiled=True),
        lax.all_gather(target, "member", axis=0, tiled=True),
    )
    grads = pair_gradient(members, everyone, all_targets, my_orders, LMAX)
    moved = lax.all_to_all(
        to_latitudes(grads, table), "space", split_axis=2, concat_axis=4, tiled=True
    )
    return to_longitudes(moved, basis)


def solution(mesh):
    placed = (P("member", None, None, "space", None), P("member", None, "space", None), P())
    return jax.shard_map(
        shards,
        mesh=mesh,
        in_specs=placed,
        out_specs=P("member", None, "space", None),
        check_vma=False,
    )
```

profile of v0, /device:TPU:0, one launch (start us, length us, event | category | flops | bytes accessed | tf_op | source)
XLA Modules:
  0.0 1374.3 jit_solution(13220429531675735985)
XLA Ops:
  16.4 616.0 %while.34 = (s32[]{:T(128)}, f32[46,368]{1,0:T(8,128)S(1)}, f32[46,368]{1,0:T(8,128)S(1)}, f32[46,368]{1,0:T(8,128)S(1)}, f32[24,16,46,368]{3,2,1,0:T(8,128)}, /...) while((s32[]{:T(128)}, f32[46,368]{1,0:T(8,128)S(1)}, ...), condition=%wide.region_1.2_spmd.clone.clone.clone.clone, body=%wide.region_0.1_spmd.clone.clone.clone.clone.sunk | while | flops 7776785 | bytes 11887176 | solution.py:66
  23.8 10.3 compare_bitcast_fusion.33
  49.4 10.3 compare_bitcast_fusion.33
  75.1 10.3 compare_bitcast_fusion.33
  100.7 10.2 compare_bitcast_fusion.33
  126.4 10.3 compare_bitcast_fusion.33
  152.1 10.3 compare_bitcast_fusion.33
  177.7 10.2 compare_bitcast_fusion.33
  203.5 10.3 compare_bitcast_fusion.33
  229.2 10.2 compare_bitcast_fusion.33
  254.8 10.2 compare_bitcast_fusion.33
  280.5 10.2 compare_bitcast_fusion.33
  306.2 10.2 compare_bitcast_fusion.33
  331.8 10.2 compare_bitcast_fusion.33
  357.5 10.2 compare_bitcast_fusion.33
  383.1 10.2 compare_bitcast_fusion.33
  408.7 10.2 compare_bitcast_fusion.33
  434.4 10.2 compare_bitcast_fusion.33
  460.0 10.2 compare_bitcast_fusion.33
  485.7 10.2 compare_bitcast_fusion.33
  511.3 10.2 compare_bitcast_fusion.33
  537.0 10.2 compare_bitcast_fusion.33
  562.7 10.2 compare_bitcast_fusion.33
  588.4 10.2 compare_bitcast_fusion.33
  614.0 10.2 compare_bitcast_fusion.33
  632.4 27.2 %copy.34 = f32[384,46,368]{0,2,1:T(8,128)} copy(f32[384,46,368]{2,1,0:T(8,128)} %bitcast.303) | data formatting | bytes 52002816 | tf_op jit(solution)/shard_map/reshape | solution.py:66
  672.8 35.1 %copy.39 = f32[16,16,2,46,384]{4,3,2,1,0:T(8,128)} copy(f32[16,16,2,46,384]{4,1,3,2,0:T(8,128)} %all-gather.5.cloned.1.call-done) | data formatting | bytes 72351744 | tf_op jit(solution)/shard_map/while | solution.py:92
  707.9 194.3 %while.33 = (s32[]{:T(128)}, f32[4,16,2,46,384]{4,3,2,1,0:T(8,128)}, f32[4,16,2,46,384]{4,1,3,2,0:T(8,128)}, f32[16,16,2,46,384]{4,3,2,1,0:T(8,128)}, s32[]{:T(128)}) while((s32[]{:T(128)}, f32[4,16,2,46,384]{4,3,2,1,0:T(8,128)}, f32[4,16,2,46,384]{4,1,3,2,0:T(8,128)}, f32[16,16,2,46,384]{4,3,2,1,0:T(8,128)}, s32[]{:T(128)}) %tuple.228), condition=%wide.region_6.7_spmd, body=%wide.region_3.6_spmd.sunk | while | flops 53698560 | bytes 165150800 | solution.py:92
  710.6 17.5 %multiply_reduce_fusion.3 = f32[16,16,46,384]{3,2,1,0:T(8,128)S(1)} fusion(f32[16,16,2,46,384]{4,3,2,1,0:T(8,128)} %get-tuple-element.1092, f32[16,2,46,384]{3,2,1,0:T(8,128)S(1)} %copy.61), kind=kLoop, calls=%fused_computation.3.clone.1 | loop fusion | flops 22609920 | bytes 56524800 | tf_op jit(solution)/shard_map/while/body/eval_jaxpr/reduce_sum | solution.py:89
  736.4 18.7 %divide_reduce_fusion.2 = f32[16,2,46,384]{3,2,1,0:T(8,128)S(1)} fusion(f32[16,16,2,46,384]{4,3,2,1,0:T(8,128)} %get-tuple-element.1092, f32[16,16,46,384]{3,2,1,0:T(8,128)} %add_sqrt_fusion.3, f32[16,2,46,384]{3,2,1,0:T(8,128)S(1)} %copy.61), kind=kLoop, calls=%fused_computation.4.clone.1 | loop fusion | flops 26566656 | bytes 58785792 | tf_op jit(solution)/shard_map/while/body/eval_jaxpr/reduce_sum | solution.py:90
  759.2 17.5 %multiply_reduce_fusion.3 = f32[16,16,46,384]{3,2,1,0:T(8,128)S(1)} fusion(f32[16,16,2,46,384]{4,3,2,1,0:T(8,128)} %get-tuple-element.1092, f32[16,2,46,384]{3,2,1,0:T(8,128)S(1)} %copy.61), kind=kLoop, calls=%fused_computation.3.clone.1 | loop fusion | flops 22609920 | bytes 56524800 | tf_op jit(solution)/shard_map/while/body/eval_jaxpr/reduce_sum | solution.py:89
  784.9 18.7 %divide_reduce_fusion.2 = f32[16,2,46,384]{3,2,1,0:T(8,128)S(1)} fusion(f32[16,16,2,46,384]{4,3,2,1,0:T(8,128)} %get-tuple-element.1092, f32[16,16,46,384]{3,2,1,0:T(8,128)} %add_sqrt_fusion.3, f32[16,2,46,384]{3,2,1,0:T(8,128)S(1)} %copy.61), kind=kLoop, calls=%fused_computation.4.clone.1 | loop fusion | flops 26566656 | bytes 58785792 | tf_op jit(solution)/shard_map/while/body/eval_jaxpr/reduce_sum | solution.py:90
  807.7 17.5 %multiply_reduce_fusion.3 = f32[16,16,46,384]{3,2,1,0:T(8,128)S(1)} fusion(f32[16,16,2,46,384]{4,3,2,1,0:T(8,128)} %get-tuple-element.1092, f32[16,2,46,384]{3,2,1,0:T(8,128)S(1)} %copy.61), kind=kLoop, calls=%fused_computation.3.clone.1 | loop fusion | flops 22609920 | bytes 56524800 | tf_op jit(solution)/shard_map/while/body/eval_jaxpr/reduce_sum | solution.py:89
  833.4 18.7 %divide_reduce_fusion.2 = f32[16,2,46,384]{3,2,1,0:T(8,128)S(1)} fusion(f32[16,16,2,46,384]{4,3,2,1,0:T(8,128)} %get-tuple-element.1092, f32[16,16,46,384]{3,2,1,0:T(8,128)} %add_sqrt_fusion.3, f32[16,2,46,384]{3,2,1,0:T(8,128)S(1)} %copy.61), kind=kLoop, calls=%fused_computation.4.clone.1 | loop fusion | flops 26566656 | bytes 58785792 | tf_op jit(solution)/shard_map/while/body/eval_jaxpr/reduce_sum | solution.py:90
  856.2 17.5 %multiply_reduce_fusion.3 = f32[16,16,46,384]{3,2,1,0:T(8,128)S(1)} fusion(f32[16,16,2,46,384]{4,3,2,1,0:T(8,128)} %get-tuple-element.1092, f32[16,2,46,384]{3,2,1,0:T(8,128)S(1)} %copy.61), kind=kLoop, calls=%fused_computation.3.clone.1 | loop fusion | flops 22609920 | bytes 56524800 | tf_op jit(solution)/shard_map/while/body/eval_jaxpr/reduce_sum | solution.py:89
  881.9 18.7 %divide_reduce_fusion.2 = f32[16,2,46,384]{3,2,1,0:T(8,128)S(1)} fusion(f32[16,16,2,46,384]{4,3,2,1,0:T(8,128)} %get-tuple-element.1092, f32[16,16,46,384]{3,2,1,0:T(8,128)} %add_sqrt_fusion.3, f32[16,2,46,384]{3,2,1,0:T(8,128)S(1)} %copy.61), kind=kLoop, calls=%fused_computation.4.clone.1 | loop fusion | flops 26566656 | bytes 58785792 | tf_op jit(solution)/shard_map/while/body/eval_jaxpr/reduce_sum | solution.py:90
  902.3 9.6 subtract_multiply_fusion
  911.8 36.6 %fusion.81 = f32[4,16,368,2,46]{2,1,3,0,4:T(8,128)} fusion(f32[4,16,2,46,384]{4,3,2,1,0:T(8,128)S(1)} %subtract_multiply_fusion, f32[384,46,368]{0,2,1:T(8,128)} %copy.34, f32[368]{0:T(512)S(1)} %copy-done.4, pred[46,384]{1,0:T(8,128)(4,1)S(1)} %copy-done.3), kind=kOutput, calls=%fused_computation.209 | convolution fusion | flops 9997541376 | bytes 43731648 | tf_op jit(solution)/shard_map/ecrml,mlj->ecjrm/dot_general | solution.py:97
  948.4 22.2 %copy.41 = f32[4,16,368,2,46]{4,1,3,0,2:T(8,128)} copy(f32[4,16,368,2,46]{2,1,3,0,4:T(8,128)} %fusion.81) | data formatting | bytes 17334272 | tf_op jit(solution)/shard_map/ecrml,mlj->ecjrm/transpose | solution.py:97
  970.6 35.0 %reshape.1226 = f32[8,1,270848]{2,1,0:T(1,128)} reshape(f32[368,4,2,16,46]{4,3,2,1,0:T(8,128)} %bitcast.300) | data formatting | bytes 17334272
  1013.1 38.5 %fusion.87 = (f32[1,368,720]{1,0,2:T(1,128)S(1)}, f32[1,368,720]{1,0,2:T(1,128)S(1)}) fusion(pred[368]{0:T(512)(128)(4,1)S(1)} %broadcast_compare_fusion, s32[368]{0:T(512)S(1)} %copy-done.5), kind=kLoop, calls=%fused_computation.214 | loop fusion | flops 3709440 | bytes 2121520 | tf_op jit(solution)/shard_map/mul | solution.py:106
  1056.4 145.8 %all-to-all-done = f32[8,1,270848]{2,1,0:T(1,128)} async-done(((f32[8,1,270848]{2,1,0:T(1,128)}), f32[8,1,270848]{2,1,0:T(1,128)}, u32[]{:S(2)}, u32[]{:S(2)}) %all-to-all-start) | async-done | bytes 8667168 | tf_op jit(solution)/shard_map/all_to_all | solution.py:138
  1202.8 27.0 %reduce = f32[8,270848]{1,0:T(8,128)} reduce(f32[8,1,270848]{2,1,0:T(1,128)} %all-to-all-done, f32[]{:T(128)} %broadcast.1891), dimensions={1}, to_apply=%all_to_all.11.reduce_sub_computation | reduce | bytes 17334276 | tf_op jit(solution)/shard_map/all_to_all | solution.py:138
  1229.7 45.5 %reshape.1227 = f32[368,4,2,16,46]{4,3,2,1,0:T(8,128)} reshape(f32[8,270848]{1,0:T(8,128)} %reduce) | data formatting | bytes 17334272
  1275.2 29.7 %copy.59 = f32[4,16,8,46,2,46]{5,2,4,1,3,0:T(8,128)} copy(f32[4,16,8,46,2,46]{5,1,4,0,3,2:T(8,128)} %bitcast.301) | data formatting | bytes 17334272 | tf_op jit(solution)/shard_map/all_to_all | solution.py:138
  1305.0 20.4 %dot_general.9 = f32[4,16,46,736]{3,1,2,0:T(8,128)} reshape(f32[4,16,46,2,8,46]{5,4,3,1,2,0:T(8,128)} %bitcast.302) | data formatting | bytes 17334272 | tf_op jit(solution)/shard_map/dot_general | solution.py:114
  1325.3 33.0 %fusion.78 = f32[4,16,46,720]{3,2,1,0:T(8,128)S(1)} fusion(f32[4,16,46,736]{3,1,2,0:T(8,128)} %dot_general.9, f32[736,720,1,1]{0,1,2,3:T(8,128)S(1)} %copy-done.1), kind=kOutput, calls=%fused_computation.201 | convolution fusion | flops 18721013760 | bytes 19265536 | tf_op jit(solution)/shard_map/dot_general | solution.py:114
  1358.4 8.8 copy.44
  (635 shorter events, 199.6 us)
Async XLA Ops:
  6.5 655.0 %all-gather.3.cloned.1.call-start = ((), (), s32[]{:S(2)}) async-start(), calls=%async_computation.1 | async-start | bytes 2826240 | tf_op jit(solution)/shard_map/all_gather | solution.py:135
  7.3 665.5 %all-gather.5.cloned.1.call-start = ((), (), s32[]{:S(2)}) async-start(), calls=%async_computation.2 | async-start | bytes 45219840 | tf_op jit(solution)/shard_map/all_gather | solution.py:134
  663.5 5.9 copy-start
  707.9 194.4 %copy-start.2 = (f32[46,384]{1,0:T(8,128)S(1)}, f32[46,384]{1,0:T(8,128)}, u32[]{:S(2)}) copy-start(f32[46,384]{1,0:T(8,128)} %fusion.93) | copy-start | bytes 211972
  902.3 9.6 copy-start.3
  902.3 9.6 copy-start.4
  1005.7 7.4 copy-start.5
  1005.7 196.5 %all-to-all-start = ((f32[8,1,270848]{2,1,0:T(1,128)}), f32[8,1,270848]{2,1,0:T(1,128)}, u32[]{:S(2)}, u32[]{:S(2)}) async-start(f32[8,1,270848]{2,1,0:T(1,128)} %reshape.1226), calls=%async_computation | async-start | bytes 17334272 | tf_op jit(solution)/shard_map/all_to_all | solution.py:138
  1305.0 20.4 %copy-start.1 = (f32[736,720,1,1]{0,1,2,3:T(8,128)S(1)}, f32[736,720,1,1]{0,1,2,3:T(8,128)}, u32[]{:S(2)}) copy-start(f32[736,720,1,1]{0,1,2,3:T(8,128)} %reshape.1221) | copy-start | bytes 6359044
Sparse Core Ops, SparseCore 0:
  8.9 26.2 all-gather.2
  36.7 218.4 all-gather.4
where the time goes:
time: 1390 us; the launch traced here: 1370 us
  other arithmetic  583 us (42%)
  local copies, waits for them, and re-layouts  298 us (21%)
  loops' own time  256 us (18%)
  waiting for transfers between devices  147 us (11%)
  matrix products  69.6 us (5%)
    another operation x1, loops' own time, legendre_table(): lax.scan(step, (zeros, zeros, zeros), jnp.arange(lpad, dtype=jnp.int32),...  255 us
    lt x24, other arithmetic, step(): degree < order_col  246 us
    all_to_all x1, waiting for transfers between devices, shards(): lax.all_to_all(to_latitudes(grads, table), 'space', split_axis=2, concat_...  146 us
    unnamed x14, local copies, waits for them, and re-layouts  80.6 us
    reduce_sum x4, other arithmetic, against(): return jnp.sum(delta / dist, axis=0)  74.8 us
    reduce_sum x4, other arithmetic, against(): dist = jnp.sqrt(jnp.sum(delta * delta, axis=2, keepdims=True) + smooth_eps)  70 us
    while x360, other arithmetic  60.1 us
    while x2, local copies, waits for them, and re-layouts, pair_gradient(): spread = lax.map(against, rows)  43.2 us
  transfers between devices with their start and end apart: 3, of which 1 were waited for; matrix products, arithmetic and copies ran while one was open for 33% of the time, Pallas kernels for 0%

commit v1 on v0

v1 whole, which is shorter than its diff:
```python
import functools
import math

import jax
import jax.numpy as jnp
from jax import lax
from jax.experimental import pallas as pl
from jax.experimental.pallas import tpu as pltpu
from jax.sharding import PartitionSpec as P


LMAX = 360
NLAT = 361
NLON = 720

EPS = 0.01
LOG_GAMMA_HALF = 0.5 * math.log(math.pi) - math.log(2.0)
STEP_EXP = 64.0
SMALL = 2.0**-64
BIG = 2.0**32
PAD = 8
VMEM_LIMIT = 60 * 1024 * 1024


def round_up(value, multiple):
    return (value + multiple - 1) // multiple * multiple


def split(value):
    high = value.astype(jnp.bfloat16)
    low = (value - high.astype(jnp.float32)).astype(jnp.bfloat16)
    return high, low


def dot(a, b, dims=(((1,), (0,)), ((), ()))):
    return lax.dot_general(a, b, dims, preferred_element_type=jnp.float32)


def table_kernel(step_ref, inv_ref, order_ref, value_ref, scale_ref, cos_ref, high_ref, low_ref, rows_ref):
    group, width = value_ref.shape
    degrees = high_ref.shape[1]
    pitch = degrees + PAD
    order = order_ref[...]
    order_sq = order * order
    cosine = jnp.broadcast_to(cos_ref[0:1, :], (group, width))

    def wide(column):
        return jnp.concatenate([column] * (width // 128), axis=1)

    order_w = wide(order)

    def factors(scale):
        one = jnp.where(scale < -0.5, jnp.where(scale < -2.5, 0.0, SMALL), 1.0)
        two = jnp.where(scale < -1.5, SMALL, 1.0)
        return one, two

    def block(index, carry):
        prev, prev2, scale, root, gap = carry
        big = (jnp.maximum(jnp.abs(prev), jnp.abs(prev2)) > BIG) & (scale < -0.5)
        prev = jnp.where(big, prev * SMALL, prev)
        prev2 = jnp.where(big, prev2 * SMALL, prev2)
        scale = jnp.where(big, scale + 1.0, scale)
        one, two = factors(scale)
        for sub in range(8):
            degree = index * 8 + sub
            deg_f = degree.astype(jnp.float32)
            gap_now = deg_f * deg_f - order_sq
            safe = jnp.maximum(gap_now, 1.0)
            root_now = lax.rsqrt(safe)
            root_now = root_now * (1.5 - 0.5 * safe * root_now * root_now)
            coef_a = step_ref[degree] * root_now
            coef_b = jnp.maximum(gap, 0.0) * root * inv_ref[degree]
            current = wide(coef_a) * (cosine * prev - wide(coef_b) * prev2)
            current = jnp.where(order_w == deg_f, value_ref[...], current)
            shown = (current * one) * two
            for first in range(0, group, 8):
                for lane in range(0, width, 128):
                    rows_ref[lane // 128, pl.ds(first * pitch + degree, 8, pitch), :] = shown[
                        first : first + 8, lane : lane + 128
                    ]
            prev2 = prev
            prev = current
            root, gap = root_now, gap_now
        return prev, prev2, scale, root, gap

    zeros = jnp.zeros((group, width), jnp.float32)
    lax.fori_loop(
        0,
        degrees // 8,
        block,
        (zeros, zeros, scale_ref[...], jnp.ones_like(order), jnp.zeros_like(order)),
    )

    def convert(index, _):
        keep = lax.broadcasted_iota(jnp.int32, (degrees, 128), 0) <= LMAX
        start = pl.multiple_of(index * pitch, 8)
        for tile in range(width // 128):
            value = jnp.where(keep, rows_ref[tile, pl.ds(start, degrees), :], 0.0)
            high, low = split(value)
            lanes = slice(tile * 128, tile * 128 + 128)
            high_ref[index, :, lanes] = high
            low_ref[index, :, lanes] = low
        return 0

    lax.fori_loop(0, group, convert, 0)


def legendre_tables(orders, degrees, lats, valid):
    count = orders.shape[0]
    width = lats.shape[0]
    span = float(NLAT - 1)
    lat_f = lats.astype(jnp.float32)
    nearest = jnp.clip(jnp.minimum(lat_f, span - lat_f), 0.0, None)
    inside = valid & (nearest > 0.0)
    sines = jnp.where(inside, jnp.sin(jnp.pi * nearest / span), 1.0)
    cosines = jnp.cos(jnp.pi * lat_f / span)
    order_f = jnp.minimum(orders, LMAX).astype(jnp.float32)
    log_base = 0.5 * (
        math.log(1.0 / (4.0 * math.pi))
        + lax.lgamma(order_f + 1.5)
        - LOG_GAMMA_HALF
        - lax.lgamma(order_f + 1.0)
    )
    start = (log_base[:, None] + order_f[:, None] * jnp.log(sines)[None, :]) / math.log(2.0)
    scale = jnp.minimum(jnp.floor(start / STEP_EXP + 0.5), 0.0)
    weight = jnp.where(orders > LMAX, 0.0, jnp.where(orders == 0, 1.0, 2.0)).astype(jnp.float32)
    value = jnp.exp2(start - STEP_EXP * scale) * jnp.where(inside, sines, 0.0)[None, :]
    value = value * weight[:, None]
    square = jnp.arange(degrees, dtype=jnp.float32) ** 2
    step = jnp.sqrt(jnp.maximum(4.0 * square - 1.0, 1.0))
    inverse = 1.0 / jnp.concatenate([jnp.ones((1,), jnp.float32), step[:-1]])
    group = 8
    order_cols = jnp.broadcast_to(order_f[:, None], (count, 128))
    cos_rows = jnp.broadcast_to(cosines[None, :], (8, width))
    rows = lambda cols: pl.BlockSpec((group, cols), lambda g, *_: (g, 0))
    out = pl.BlockSpec((group, degrees, width), lambda g, *_: (g, 0, 0))
    shape = jax.ShapeDtypeStruct((count, degrees, width), jnp.bfloat16)
    return pl.pallas_call(
        table_kernel,
        name="legendre_table",
        out_shape=(shape, shape),
        grid_spec=pltpu.PrefetchScalarGridSpec(
            num_scalar_prefetch=2,
            grid=(count // group,),
            in_specs=[rows(128), rows(width), rows(width), pl.BlockSpec((8, width), lambda g, *_: (0, 0))],
            out_specs=(out, out),
            scratch_shapes=[pltpu.VMEM((width // 128, group * (degrees + PAD), 128), jnp.float32)],
        ),
        compiler_params=pltpu.CompilerParams(vmem_limit_bytes=VMEM_LIMIT),
        cost_estimate=pl.CostEstimate(
            flops=10 * count * degrees * width,
            transcendentals=count * degrees,
            bytes_accessed=4 * count * degrees * width,
        ),
    )(step, inverse, order_cols, value, scale, cos_rows)


def gradient_kernel(slots, me_ref, *refs):
    blocks = refs[:-8]
    target_ref, high_ref, low_ref, band_ref, out_ref, sums_ref, grads_ref, lat_ref = refs[-8:]
    groups = len(blocks)
    local = blocks[0].shape[0]
    degrees = target_ref.shape[2]
    width = high_ref.shape[2]
    spaces = out_ref.shape[1]
    width_out = out_ref.shape[3]
    count = groups * local
    rows = 2 * count
    pitch = rows + PAD
    per = 2 * local
    lanes_of = width // spaces
    first_slot = pl.program_id(0) * 8
    live = lax.broadcasted_iota(jnp.int32, (8, 128), 0) + first_slot < slots
    share = 1.0 / count
    pair_share = 1.0 / (count * (count - 1))

    def lane_tile(tile, _):
        lanes = pl.ds(pl.multiple_of(tile * 128, 128), 128)

        def coef(index):
            ref = blocks[index // local]
            return ref[index % local, 0, :, lanes], ref[index % local, 1, :, lanes]

        for group in range(groups):
            base = group * local
            mine = [coef(base + e) for e in range(local)]
            if group == 0:
                total = [[jnp.zeros((8, 128), jnp.float32) for _ in range(2)] for _ in range(local)]
            else:
                total = [[sums_ref[2 * (base + e) + r] for r in range(2)] for e in range(local)]

            def force(a, b):
                real, imag = a[0] - b[0], a[1] - b[1]
                inverse = lax.rsqrt(real * real + (imag * imag + EPS))
                return real * inverse, imag * inverse

            for e in range(local):
                for f in range(e + 1, local):
                    pull = force(mine[e], mine[f])
                    for r in range(2):
                        total[e][r] = total[e][r] + pull[r]
                        total[f][r] = total[f][r] - pull[r]
            for other in range(base + local, count):
                theirs = coef(other)
                sums = None if group == 0 else [sums_ref[2 * other + r] for r in range(2)]
                for e in range(local):
                    pull = force(mine[e], theirs)
                    for r in range(2):
                        total[e][r] = total[e][r] + pull[r]
                    if sums is None:
                        sums = [-pull[0], -pull[1]]
                    else:
                        sums = [sums[0] - pull[0], sums[1] - pull[1]]
                for r in range(2):
                    sums_ref[2 * other + r] = sums[r]
            goal = (target_ref[0, :, lanes], target_ref[1, :, lanes])
            owner = lax.rem(me_ref[0] + (groups - group), groups)
            for e in range(local):
                pull = force(mine[e], goal)
                for r in range(2):
                    grad = pull[r] * share - total[e][r] * pair_share
                    grad = jnp.where(live, grad, 0.0)
                    grads_ref[tile, pl.ds(owner * per + r * local + e, 8, pitch), :] = grad
        return 0

    lax.fori_loop(0, degrees // 128, lane_tile, 0)

    def transform(slot, _):
        start = pl.multiple_of(slot * pitch, 8)
        grad = jnp.concatenate(
            [grads_ref[tile, pl.ds(start, rows), :] for tile in range(degrees // 128)], axis=1
        )
        high, low = split(grad)
        both = dot(jnp.concatenate([high, low], axis=0), high_ref[slot])
        lat = both[:rows] + both[rows:] + dot(high, low_ref[slot])
        for tile in range(width // 128):
            lat_ref[tile, pl.ds(start, rows), :] = lat[:, tile * 128 : tile * 128 + 128]
        return 0

    lax.fori_loop(0, 8, transform, 0, unroll=2)

    band = band_ref[...]

    def load(group, row):
        parts = [
            lat_ref[tile, pl.ds(group * per + row, 8, pitch), :] for tile in range(width // 128)
        ]
        return jnp.concatenate(parts, axis=1)

    def scatter(group, _):
        source = [load(group, row) for row in range(per)]
        if spaces == per and width == width_out:
            distance = per // 2
            while distance:
                upper = (band & distance) != 0
                for i in range(per):
                    if i & distance:
                        continue
                    j = i | distance
                    shift = distance * lanes_of
                    from_j = pltpu.roll(source[j], shift, 1)
                    from_i = pltpu.roll(source[i], width - shift, 1)
                    source[i], source[j] = (
                        jnp.where(upper, from_j, source[i]),
                        jnp.where(upper, source[j], from_i),
                    )
                distance //= 2
            for space in range(spaces):
                out_ref[group, space] = source[space]
        else:
            for space in range(spaces):
                value = jnp.zeros((8, width_out), jnp.float32)
                for row in range(per):
                    shift = (row - space) * lanes_of % width
                    moved = source[row] if shift == 0 else pltpu.roll(source[row], shift, 1)
                    value = jnp.where(band[:, :width_out] == row, moved[:, :width_out], value)
                out_ref[group, space] = value
        return 0

    lax.fori_loop(0, groups, scatter, 0)


def lat_payload(me, parts, targets, channel, high, low, spaces):
    local, _, slots, degrees = parts[0].shape
    groups = len(parts)
    padded, _, width = high.shape
    per = 2 * local
    lanes_of = width // spaces
    width_out = round_up(per * lanes_of, 128)
    count = groups * local
    band = jnp.broadcast_to((jnp.arange(width, dtype=jnp.int32) // lanes_of)[None], (8, width))
    part_spec = pl.BlockSpec((local, 2, 8, degrees), lambda g, *_: (0, 0, g, 0))
    table_spec = pl.BlockSpec((8, degrees, width), lambda g, *_: (g, 0, 0))
    pairs = count * (count + 1) // 2
    return pl.pallas_call(
        functools.partial(gradient_kernel, slots),
        name="loss_gradient",
        out_shape=jax.ShapeDtypeStruct((groups, spaces, padded, width_out), jnp.float32),
        grid_spec=pltpu.PrefetchScalarGridSpec(
            num_scalar_prefetch=1,
            grid=(padded // 8,),
            in_specs=[part_spec] * groups
            + [
                pl.BlockSpec((None, 2, 8, degrees), lambda g, *_: (channel, 0, g, 0)),
                table_spec,
                table_spec,
                pl.BlockSpec((8, width), lambda g, *_: (0, 0)),
            ],
            out_specs=pl.BlockSpec((groups, spaces, 8, width_out), lambda g, *_: (0, 0, g, 0)),
            scratch_shapes=[
                pltpu.VMEM((2 * count, 8, 128), jnp.float32),
                pltpu.VMEM((degrees // 128, 8 * (2 * count + PAD), 128), jnp.float32),
                pltpu.VMEM((width // 128, 8 * (2 * count + PAD), 128), jnp.float32),
            ],
        ),
        compiler_params=pltpu.CompilerParams(vmem_limit_bytes=VMEM_LIMIT),
        cost_estimate=pl.CostEstimate(
            flops=6 * 2 * count * padded * degrees * width,
            transcendentals=pairs * padded * degrees,
            bytes_accessed=4 * padded * degrees * width + 16 * count * padded * degrees,
        ),
    )(me, *parts, targets, high, low, band)


def longitude_kernel(got_ref, high_ref, low_ref, out_ref):
    half = out_ref.shape[0]
    value = got_ref[...].T
    both = jnp.concatenate([value[:half], value[half : 2 * half]], axis=1)
    high, low = split(both)
    out_ref[...] = (
        dot(high, high_ref[...]) + dot(low, high_ref[...]) + dot(high, low_ref[...])
    )


def to_longitudes(received, high, low, half):
    groups, depth, width = received.shape
    whole = lambda shape: pl.BlockSpec(shape, lambda g: (0, 0))
    return pl.pallas_call(
        longitude_kernel,
        name="longitudes",
        out_shape=jax.ShapeDtypeStruct((groups, half, NLON), jnp.float32),
        grid=(groups,),
        in_specs=[
            pl.BlockSpec((None, depth, width), lambda g: (g, 0, 0)),
            whole(high.shape),
            whole(low.shape),
        ],
        out_specs=pl.BlockSpec((None, half, NLON), lambda g: (g, 0, 0)),
        compiler_params=pltpu.CompilerParams(vmem_limit_bytes=VMEM_LIMIT),
        cost_estimate=pl.CostEstimate(
            flops=6 * groups * half * 2 * depth * NLON,
            transcendentals=0,
            bytes_accessed=4 * groups * (depth * width + half * NLON),
        ),
    )(received, high, low)


def merge_kernel(lats, *refs):
    ins, out_ref, wide_ref = refs[:-2], refs[-2], refs[-1]
    chunks = len(ins)
    groups = ins[0].shape[0]
    channels = groups * chunks
    padded = ins[0].shape[1]
    pitch = channels + PAD
    for group in range(groups):
        for chunk in range(chunks):
            channel = group * chunks + chunk
            for first in range(0, padded, 8):
                for lane in range(0, NLON, 128):
                    size = min(128, NLON - lane)
                    value = ins[chunk][group, first : first + 8, lane : lane + size]
                    if size < 128:
                        value = jnp.concatenate([value, jnp.zeros((8, 128 - size), jnp.float32)], axis=1)
                    wide_ref[lane // 128, pl.ds(first * pitch + channel, 8, pitch), :] = value
    for lane in range(0, NLON, 128):
        size = min(128, NLON - lane)
        for lat in range(lats):
            out_ref[lat * channels : (lat + 1) * channels, lane : lane + size] = wide_ref[
                lane // 128, lat * pitch : lat * pitch + channels, :size
            ]


def merge(parts, local, lats, lanes_of):
    groups = parts[0].shape[0]
    channels = groups * len(parts)
    padded = round_up(lanes_of, 8)
    parts = [
        part if padded == lanes_of else jnp.pad(
            part.reshape(groups, local, lanes_of, NLON), ((0, 0), (0, 0), (0, padded - lanes_of), (0, 0))
        ).reshape(groups, local * padded, NLON)
        for part in parts
    ]
    out = pl.pallas_call(
        functools.partial(merge_kernel, lats),
        name="merge_channels",
        out_shape=jax.ShapeDtypeStruct((local, lats * channels, NLON), jnp.float32),
        grid=(local,),
        in_specs=[pl.BlockSpec((groups, padded, NLON), lambda e: (0, e, 0))] * len(parts),
        out_specs=pl.BlockSpec((None, lats * channels, NLON), lambda e: (e, 0, 0)),
        scratch_shapes=[pltpu.VMEM((pl.cdiv(NLON, 128), padded * (channels + PAD), 128), jnp.float32)],
        compiler_params=pltpu.CompilerParams(vmem_limit_bytes=VMEM_LIMIT),
        cost_estimate=pl.CostEstimate(
            flops=0, transcendentals=0, bytes_accessed=8 * local * lats * channels * NLON
        ),
    )(*parts)
    return out.reshape(local, lats, channels, NLON).transpose(0, 2, 1, 3)


def longitude_basis(orders):
    cols = jnp.arange(NLON, dtype=jnp.int32)
    phase = orders[:, None] * cols[None, :] % NLON
    angle = 2.0 * jnp.pi * phase.astype(jnp.float32) / NLON
    valid = (orders <= LMAX)[:, None]
    scale = 2.0 * jnp.pi / NLON
    cosine = jnp.where(valid, jnp.cos(angle), 0.0) * scale
    sine = jnp.where(valid, -jnp.sin(angle), 0.0) * scale
    value = jnp.concatenate([cosine, sine], axis=0)
    high = lax.reduce_precision(value, 8, 7)
    return high.astype(jnp.bfloat16), (value - high).astype(jnp.bfloat16)


def shards(members, target, order_table):
    local, channels, _, slots, degrees = members.shape
    spaces = lax.axis_size("space")
    groups = lax.axis_size("member")
    chunks = channels // groups
    me = lax.axis_index("member")
    padded = round_up(slots, 16)
    lats = (NLAT + spaces - 1) // spaces
    width = round_up(spaces * lats, 128)
    lanes_of = width // spaces

    by_device = jnp.pad(
        order_table.reshape(spaces, slots), ((0, 0), (0, padded - slots)), constant_values=LMAX + 1
    )
    mine = lax.dynamic_index_in_dim(by_device, lax.axis_index("space"), 0, keepdims=False)
    column = jnp.arange(width, dtype=jnp.int32)
    inner = column % lanes_of
    lat_index = column // lanes_of * lats + inner
    valid = (inner < lats) & (lat_index < NLAT)

    def pieces(source, chunk):
        result = []
        for step in range(groups):
            channel = lax.rem(me + step, groups) * chunks + chunk
            result.append(lax.dynamic_index_in_dim(source, channel, 1, keepdims=False))
        return result

    def exchange(cut):
        return [cut[0]] + [
            lax.ppermute(cut[step], "member", [(i, (i + step) % groups) for i in range(groups)])
            for step in range(1, groups)
        ]

    high, low = legendre_tables(mine, degrees, jnp.where(valid, lat_index, 0), valid)
    basis_high, basis_low = longitude_basis(by_device.reshape(-1))
    index = me.reshape(1).astype(jnp.int32)
    arrived = []
    outputs = []
    for chunk in range(chunks):
        source = members
        if chunk:
            source, *arrived[chunk - 1] = lax.optimization_barrier((source, *arrived[chunk - 1]))
        arrived.append(exchange(pieces(source, chunk)))
    for chunk in range(chunks):
        parts = arrived[chunk]
        payload = lat_payload(index, parts, target, chunk, high, low, spaces)
        blocks = payload.reshape(groups * spaces, padded, payload.shape[3])
        moved = lax.all_to_all(blocks, ("member", "space"), 0, 0, tiled=True)
        moved = moved.reshape(groups, spaces * padded, payload.shape[3])
        outputs.append(to_longitudes(moved, basis_high, basis_low, local * lanes_of))
    return merge(outputs, local, lats, lanes_of)


def solution(mesh):
    placed = (P("member", None, None, "space", None), P("member", None, "space", None), P())

    return jax.shard_map(
        shards,
        mesh=mesh,
        in_specs=placed,
        out_specs=P("member", None, "space", None),
        check_vma=False,
    )
```

time: 1390 us -> 390 us (0.28); the launches traced: 1370 us -> 389 us
  other arithmetic: 583 us -> 8.65 us
  local copies, waits for them, and re-layouts: 298 us -> 32.7 us
  loops' own time: 256 us -> 0 us
  Pallas kernels: 0 us -> 149 us
  matrix products: 69.6 us -> 0 us
  starting transfers between devices: 7.46 us -> 50.9 us
    another operation x2 -> x0, loops' own time: 256 us -> none  [the longest x1 255 us: legendre_table(): lax.scan(step, (zeros, zeros, zeros), jnp.arange(lpad, dtype=jnp.int32),...]
    lt x24 -> x0, other arithmetic: 246 us -> none  [step(): degree < order_col]
    reduce_sum x9 -> x0, other arithmetic: 151 us -> none  [the longest x4 74.8 us: against(): return jnp.sum(delta / dist, axis=0)]
    pallas_call x0 -> x10, Pallas kernels: none -> 149 us  [the longest x4 88.8 us: lat_payload(): pl.pallas_call(functools.partial(gradient_kernel, slots), name='loss_grad...]
    ppermute x0 -> x12, waiting for transfers between devices: none -> 120 us  [exchange(): lax.ppermute(cut[step], 'member', [(i, (i + step) % groups) for i in rang...]
    all_to_all x1 -> x4, waiting for transfers between devices: 146 us -> 27.7 us  [shards(): moved = lax.all_to_all(blocks, ('member', 'space'), 0, 0, tiled=True)]
    unnamed x14 -> x11, local copies, waits for them, and re-layouts: 80.6 us -> 3.79 us
    dot_general x2 -> x0, matrix products: 69.6 us -> none  [the longest x1 36.6 us: to_latitudes(): jnp.einsum('ecrml,mlj->ecjrm', grads, table, precision=lax.Precision.HIGH...]
  transfers between devices with their start and end apart: 3 -> 16, of which waited for: 1 -> 10; matrix products, arithmetic and copies ran while one was open for 33% -> 8% of each run, Pallas kernels for 0% -> 29%
where the time goes in v1:
time: 390 us; the launch traced here: 389 us
  Pallas kernels  149 us (38%)
  waiting for transfers between devices  148 us (38%)
  starting transfers between devices  50.9 us (13%)
  local copies, waits for them, and re-layouts  32.7 us (8%)
  other arithmetic  8.65 us (2%)
    ppermute x12, waiting for transfers between devices, exchange(): lax.ppermute(cut[step], 'member', [(i, (i + step) % groups) for i in rang...  120 us
    pallas_call x4, Pallas kernels, lat_payload(): pl.pallas_call(functools.partial(gradient_kernel, slots), name='loss_grad...  88.8 us
    all_to_all x4, starting transfers between devices, shards(): moved = lax.all_to_all(blocks, ('member', 'space'), 0, 0, tiled=True)  36.6 us
    pallas_call x4, Pallas kernels, to_longitudes(): pl.pallas_call(longitude_kernel, name='longitudes', out_shape=jax.ShapeDt...  27.7 us
    all_to_all x4, waiting for transfers between devices, shards(): moved = lax.all_to_all(blocks, ('member', 'space'), 0, 0, tiled=True)  27.7 us
    pallas_call x1, Pallas kernels, legendre_tables(): pl.pallas_call(table_kernel, name='legendre_table', out_shape=(shape, sha...  23.9 us
    dynamic_slice x20, local copies, waits for them, and re-layouts, pieces(): result.append(lax.dynamic_index_in_dim(source, channel, 1, keepdims=False))  16.3 us
    ppermute x12, starting transfers between devices, exchange(): lax.ppermute(cut[step], 'member', [(i, (i + step) % groups) for i in rang...  14.3 us
  transfers between devices with their start and end apart: 16, of which 10 were waited for; matrix products, arithmetic and copies ran while one was open for 8% of the time, Pallas kernels for 29%

profile of v1, /device:TPU:0, one launch (start us, length us, event | category | flops | bytes accessed | tf_op | source)
XLA Modules:
  0.0 389.4 jit_solution(3342530810215352585)
XLA Ops:
  0.0 2.3 constant_dynamic-slice_fusion.13
  3.1 1.0 copy.86
  4.0 2.5 collective-permute-start.1
  6.5 1.0 copy.85
  7.5 1.5 collective-permute-start.2
  9.1 0.9 copy.31.refs_4_
  13.8 23.9 %legendre_table.1 = (bf16[48,384,384]{2,1,0:T(8,128)(2,1)}, bf16[48,384,384]{2,1,0:T(8,128)(2,1)}) custom-call(f32[384]{0:T(512)} %copy-done.3, f32[384]{0:T(512)} %maximum_divide_fusion.inv_ref, f32[48,128]{1,0:T(8,128)} %broadcast_in_dim.39.order_ref, f32[48,384]{1,0:T(8,128)} %get-tuple-element.60.value_ref, f32[48,384]{1,0:T(8,128)} %get-tuple-element.59.scale_ref, ...), custom_call_target="tpu_custom_call" | custom-call | flops 70778880 | bytes 28311552 | tf_op jit(solution)/shard_map/legendre_table/pallas_call | solution.py:138
  38.6 0.9 copy.29.refs_2_
  39.5 0.9 copy.30.refs_3_
  41.0 22.2 %loss_gradient.4 = f32[4,8,48,384]{3,2,1,0:T(8,128)} custom-call(s32[1]{0:T(128)} %bitcast.me_ref, f32[4,2,46,384]{3,2,1,0:T(8,128)} %bitcast.72, f32[4,2,46,384]{3,2,1,0:T(8,128)} %copy.28.refs_1_, f32[4,2,46,384]{3,2,1,0:T(8,128)} %copy.29.refs_2_, f32[4,2,46,384]{3,2,1,0:T(8,128)} %copy.30.refs_3_, f32[4,2,46,384]{3,2,1,0:T(8,128)} %copy.31.refs_4_, ...), custom_call_target="tpu_custom_call" | custom-call | flops 1358954496 | bytes 33030144 | tf_op jit(solution)/shard_map/loss_gradient/pallas_call | solution.py:295
  63.1 4.9 %all-to-all-start = ((f32[32,48,384]{2,1,0:T(8,128)}), f32[32,48,384]{2,1,0:T(8,128)S(1)}, u32[]{:S(2)}, u32[]{:S(2)}) async-start(f32[32,48,384]{2,1,0:T(8,128)} %bitcast.68), calls=%async_computation | async-start | bytes 4718592 | tf_op jit(solution)/shard_map/all_to_all | solution.py:469
  68.1 2.4 constant_dynamic-slice_fusion.8
  71.2 1.6 collective-permute-start.4
  72.9 1.4 collective-permute-start.5
  75.1 27.1 %collective-permute-done.3 = f32[4,2,46,384]{3,0,2,1:T(4,128)S(1)} collective-permute-done((f32[4,2,46,384]{3,0,2,1:T(4,128)S(1)}, f32[4,2,46,384]{3,0,2,1:T(4,128)S(1)}, u32[]{:S(2)}, u32[]{:S(2)}) %collective-permute-start.3) | collective-permute-done | bytes 565280 | tf_op jit(solution)/shard_map/ppermute | solution.py:451
  102.2 1.6 collective-permute-done.4
  103.8 11.9 %collective-permute-done.5 = f32[4,2,46,384]{3,0,2,1:T(4,128)S(1)} collective-permute-done((f32[4,2,46,384]{3,0,2,1:T(4,128)S(1)}, f32[4,2,46,384]{3,0,2,1:T(4,128)S(1)}, u32[]{:S(2)}, u32[]{:S(2)}) %collective-permute-start.5) | collective-permute-done | bytes 565280 | tf_op jit(solution)/shard_map/ppermute | solution.py:451
  116.6 0.9 copy.37.refs_2_
  117.5 0.9 copy.38.refs_3_
  118.4 22.2 %loss_gradient.5 = f32[4,8,48,384]{3,2,1,0:T(8,128)} custom-call(s32[1]{0:T(128)} %bitcast.me_ref, f32[4,2,46,384]{3,2,1,0:T(8,128)} %bitcast.74, f32[4,2,46,384]{3,2,1,0:T(8,128)} %copy.36.refs_1_, f32[4,2,46,384]{3,2,1,0:T(8,128)} %copy.37.refs_2_, f32[4,2,46,384]{3,2,1,0:T(8,128)} %copy.38.refs_3_, f32[4,2,46,384]{3,2,1,0:T(8,128)} %copy.31.refs_4_, ...), custom_call_target="tpu_custom_call" | custom-call | flops 1358954496 | bytes 33030144 | tf_op jit(solution)/shard_map/loss_gradient/pallas_call | solution.py:295
  140.6 1.4 copy-done
  142.0 10.4 %all-to-all-start.1 = ((f32[32,48,384]{2,1,0:T(8,128)}), f32[32,48,384]{2,1,0:T(8,128)}, u32[]{:S(2)}, u32[]{:S(2)}) async-start(f32[32,48,384]{2,1,0:T(8,128)} %bitcast.67), calls=%async_computation.1 | async-start | bytes 4718592 | tf_op jit(solution)/shard_map/all_to_all | solution.py:469
  152.5 2.4 constant_dynamic-slice_fusion.4
  155.5 1.6 collective-permute-start.7
  157.2 1.4 collective-permute-start.8
  159.4 27.1 %collective-permute-done.6 = f32[4,2,46,384]{3,0,2,1:T(4,128)S(1)} collective-permute-done((f32[4,2,46,384]{3,0,2,1:T(4,128)S(1)}, f32[4,2,46,384]{3,0,2,1:T(4,128)S(1)}, u32[]{:S(2)}, u32[]{:S(2)}) %collective-permute-start.6) | collective-permute-done | bytes 565280 | tf_op jit(solution)/shard_map/ppermute | solution.py:451
  186.4 1.6 collective-permute-done.7
  188.1 11.9 %collective-permute-done.8 = f32[4,2,46,384]{3,0,2,1:T(4,128)S(1)} collective-permute-done((f32[4,2,46,384]{3,0,2,1:T(4,128)S(1)}, f32[4,2,46,384]{3,0,2,1:T(4,128)S(1)}, u32[]{:S(2)}, u32[]{:S(2)}) %collective-permute-start.8) | collective-permute-done | bytes 565280 | tf_op jit(solution)/shard_map/ppermute | solution.py:451
  201.7 0.9 copy.46.refs_3_
  202.6 22.2 %loss_gradient.6 = f32[4,8,48,384]{3,2,1,0:T(8,128)} custom-call(s32[1]{0:T(128)} %bitcast.me_ref, f32[4,2,46,384]{3,2,1,0:T(8,128)} %bitcast.75, f32[4,2,46,384]{3,2,1,0:T(8,128)} %copy.44.refs_1_, f32[4,2,46,384]{3,2,1,0:T(8,128)} %copy.45.refs_2_, f32[4,2,46,384]{3,2,1,0:T(8,128)} %copy.46.refs_3_, f32[4,2,46,384]{3,2,1,0:T(8,128)} %copy.31.refs_4_, ...), custom_call_target="tpu_custom_call" | custom-call | flops 1358954496 | bytes 33030144 | tf_op jit(solution)/shard_map/loss_gradient/pallas_call | solution.py:295
  224.8 10.3 %all-to-all-start.2 = ((f32[32,48,384]{2,1,0:T(8,128)}), f32[32,48,384]{2,1,0:T(8,128)S(1)}, u32[]{:S(2)}, u32[]{:S(2)}) async-start(f32[32,48,384]{2,1,0:T(8,128)} %bitcast.66), calls=%async_computation.2 | async-start | bytes 4718592 | tf_op jit(solution)/shard_map/all_to_all | solution.py:469
  235.2 2.4 constant_dynamic-slice_fusion
  238.3 1.6 collective-permute-start.10
  239.9 1.4 collective-permute-start.11
  242.1 27.1 %collective-permute-done.9 = f32[4,2,46,384]{3,0,2,1:T(4,128)S(1)} collective-permute-done((f32[4,2,46,384]{3,0,2,1:T(4,128)S(1)}, f32[4,2,46,384]{3,0,2,1:T(4,128)S(1)}, u32[]{:S(2)}, u32[]{:S(2)}) %collective-permute-start.9) | collective-permute-done | bytes 565280 | tf_op jit(solution)/shard_map/ppermute | solution.py:451
  271.8 11.0 %collective-permute-done.11 = f32[4,2,46,384]{3,0,2,1:T(4,128)S(1)} collective-permute-done((f32[4,2,46,384]{3,0,2,1:T(4,128)S(1)}, f32[4,2,46,384]{3,0,2,1:T(4,128)S(1)}, u32[]{:S(2)}, u32[]{:S(2)}) %collective-permute-start.11) | collective-permute-done | bytes 565280 | tf_op jit(solution)/shard_map/ppermute | solution.py:451
  282.8 0.9 copy.54.refs_3_
  283.7 22.2 %loss_gradient.7 = f32[4,8,48,384]{3,2,1,0:T(8,128)} custom-call(s32[1]{0:T(128)} %bitcast.me_ref, f32[4,2,46,384]{3,2,1,0:T(8,128)} %bitcast.73, f32[4,2,46,384]{3,2,1,0:T(8,128)} %copy.52.refs_1_, f32[4,2,46,384]{3,2,1,0:T(8,128)} %copy.53.refs_2_, f32[4,2,46,384]{3,2,1,0:T(8,128)} %copy.54.refs_3_, f32[4,2,46,384]{3,2,1,0:T(8,128)} %copy.31.refs_4_, ...), custom_call_target="tpu_custom_call" | custom-call | flops 1358954496 | bytes 33030144 | tf_op jit(solution)/shard_map/loss_gradient/pallas_call | solution.py:295
  305.9 1.5 copy-done.1
  307.4 11.0 %all-to-all-start.3 = ((f32[32,48,384]{2,1,0:T(8,128)}), f32[32,48,384]{2,1,0:T(8,128)}, u32[]{:S(2)}, u32[]{:S(2)}) async-start(f32[32,48,384]{2,1,0:T(8,128)} %bitcast.69), calls=%async_computation.3 | async-start | bytes 4718592 | tf_op jit(solution)/shard_map/all_to_all | solution.py:469
  318.5 5.2 %select_multiply_fusion.1 = (f32[384,720]{1,0:T(8,128)S(1)}, f32[384,720]{1,0:T(8,128)S(1)}) fusion(s32[384]{0:T(512)S(1)} %reshape.237, pred[384]{0:T(512)(128)(4,1)S(1)} %broadcast_compare_fusion), kind=kLoop, calls=%fused_computation.8 | loop fusion | flops 3870720 | bytes 2213760 | tf_op jit(solution)/shard_map/mul | solution.py:415
  323.7 1.8 fusion
  325.4 6.9 %longitudes.4.refs_0_ = f32[4,192,720]{2,1,0:T(8,128)} custom-call(f32[4,384,384]{2,1,0:T(8,128)} %bitcast.70, bf16[768,720]{1,0:T(8,128)(2,1)} %get-tuple-element.58.high_ref, bf16[768,720]{1,0:T(8,128)(2,1)} %get-tuple-element.57.low_ref), custom_call_target="tpu_custom_call" | custom-call | flops 2548039680 | bytes 4571136 | tf_op jit(solution)/shard_map/longitudes/pallas_call | solution.py:338
  332.4 7.0 %longitudes.5.refs_1_ = f32[4,192,720]{2,1,0:T(8,128)} custom-call(f32[4,384,384]{2,1,0:T(8,128)} %bitcast.14.got_ref, bf16[768,720]{1,0:T(8,128)(2,1)} %get-tuple-element.58.high_ref, bf16[768,720]{1,0:T(8,128)(2,1)} %get-tuple-element.57.low_ref), custom_call_target="tpu_custom_call" | custom-call | flops 2548039680 | bytes 4571136 | tf_op jit(solution)/shard_map/longitudes/pallas_call | solution.py:338
  339.3 6.9 %longitudes.6.refs_2_ = f32[4,192,720]{2,1,0:T(8,128)} custom-call(f32[4,384,384]{2,1,0:T(8,128)} %bitcast.71, bf16[768,720]{1,0:T(8,128)(2,1)} %get-tuple-element.58.high_ref, bf16[768,720]{1,0:T(8,128)(2,1)} %get-tuple-element.57.low_ref), custom_call_target="tpu_custom_call" | custom-call | flops 2548039680 | bytes 4571136 | tf_op jit(solution)/shard_map/longitudes/pallas_call | solution.py:338
  346.2 27.7 %all-to-all-done.3 = f32[32,48,384]{2,1,0:T(8,128)} async-done(((f32[32,48,384]{2,1,0:T(8,128)}), f32[32,48,384]{2,1,0:T(8,128)}, u32[]{:S(2)}, u32[]{:S(2)}) %all-to-all-start.3) | async-done | bytes 2359328 | tf_op jit(solution)/shard_map/all_to_all | solution.py:469
  373.9 6.9 %longitudes.7.refs_3_ = f32[4,192,720]{2,1,0:T(8,128)} custom-call(f32[4,384,384]{2,1,0:T(8,128)} %bitcast.26.got_ref, bf16[768,720]{1,0:T(8,128)(2,1)} %get-tuple-element.58.high_ref, bf16[768,720]{1,0:T(8,128)(2,1)} %get-tuple-element.57.low_ref), custom_call_target="tpu_custom_call" | custom-call | flops 2548039680 | bytes 4571136 | tf_op jit(solution)/shard_map/longitudes/pallas_call | solution.py:338
  380.8 8.6 %merge_channels.1 = f32[4,736,720]{2,1,0:T(8,128)} custom-call(f32[4,192,720]{2,1,0:T(8,128)} %longitudes.4.refs_0_, f32[4,192,720]{2,1,0:T(8,128)} %longitudes.5.refs_1_, f32[4,192,720]{2,1,0:T(8,128)} %longitudes.6.refs_2_, f32[4,192,720]{2,1,0:T(8,128)} %longitudes.7.refs_3_), custom_call_target="tpu_custom_call" | custom-call | bytes 16957440 | tf_op jit(solution)/shard_map/merge_channels/pallas_call | solution.py:393
  (54 shorter events, 16.1 us)
Async XLA Ops:
  2.5 6.5 %copy-start.4 = (s32[368]{0:T(512)S(1)}, s32[368]{0:T(512)}, u32[]{:S(2)}) copy-start(s32[368]{0:T(512)} %param.5) | copy-start | bytes 4420
  2.5 6.6 %copy-start.2 = (f32[4,2,46,384]{3,1,2,0:T(2,128)S(1)}, f32[4,2,46,384]{3,1,2,0:T(2,128)}, u32[]{:S(2)}) copy-start(f32[4,2,46,384]{3,1,2,0:T(2,128)} %param.4) | copy-start | bytes 1695748
  2.5 35.2 %collective-permute-start = (f32[4,2,46,384]{3,0,2,1:T(4,128)S(1)}, f32[4,2,46,384]{3,0,2,1:T(4,128)S(1)}, u32[]{:S(2)}, u32[]{:S(2)}) collective-permute-start(f32[4,2,46,384]{3,0,2,1:T(4,128)S(1)} %bitcast.76), channel_id=1, source_target_pairs={{0,8},{8,16},{16,24},{24,0},{1,9},{9,17},{17,25},{25,1},{2,10},{10... | collective-permute-start | bytes 1695752 | tf_op jit(solution)/shard_map/ppermute | solution.py:451
  4.0 33.7 %collective-permute-start.1 = (f32[4,2,46,384]{3,0,2,1:T(4,128)}, f32[4,2,46,384]{3,0,2,1:T(4,128)S(1)}, u32[]{:S(2)}, u32[]{:S(2)}) collective-permute-start(f32[4,2,46,384]{3,0,2,1:T(4,128)} %bitcast.63), channel_id=1, source_target_pairs={{0,16},{8,24},{16,0},{24,8},{1,17},{9,25},{17,1},{25,9},{2,18},{10... | collective-permute-start | bytes 1695752 | tf_op jit(solution)/shard_map/ppermute | solution.py:451
  7.5 30.2 %collective-permute-start.2 = (f32[4,2,46,384]{3,0,2,1:T(4,128)}, f32[4,2,46,384]{3,0,2,1:T(4,128)S(1)}, u32[]{:S(2)}, u32[]{:S(2)}) collective-permute-start(f32[4,2,46,384]{3,0,2,1:T(4,128)} %bitcast.62), channel_id=1, source_target_pairs={{0,24},{8,0},{16,8},{24,16},{1,25},{9,1},{17,9},{25,17},{2,26},{10... | collective-permute-start | bytes 1695752 | tf_op jit(solution)/shard_map/ppermute | solution.py:451
  9.0 3.5 copy-start.3
  63.1 77.5 %all-to-all-start = ((f32[32,48,384]{2,1,0:T(8,128)}), f32[32,48,384]{2,1,0:T(8,128)S(1)}, u32[]{:S(2)}, u32[]{:S(2)}) async-start(f32[32,48,384]{2,1,0:T(8,128)} %bitcast.68), calls=%async_computation | async-start | bytes 4718592 | tf_op jit(solution)/shard_map/all_to_all | solution.py:469
  70.9 31.3 %collective-permute-start.3 = (f32[4,2,46,384]{3,0,2,1:T(4,128)S(1)}, f32[4,2,46,384]{3,0,2,1:T(4,128)S(1)}, u32[]{:S(2)}, u32[]{:S(2)}) collective-permute-start(f32[4,2,46,384]{3,0,2,1:T(4,128)S(1)} %bitcast.83), channel_id=1, source_target_pairs={{0,8},{8,16},{16,24},{24,0},{1,9},{9,17},{17,25},{25,1},{2,10},{10... | collective-permute-start | bytes 1695752 | tf_op jit(solution)/shard_map/ppermute | solution.py:451
  71.2 32.6 %collective-permute-start.4 = (f32[4,2,46,384]{3,0,2,1:T(4,128)S(1)}, f32[4,2,46,384]{3,0,2,1:T(4,128)S(1)}, u32[]{:S(2)}, u32[]{:S(2)}) collective-permute-start(f32[4,2,46,384]{3,0,2,1:T(4,128)S(1)} %bitcast.81), channel_id=1, source_target_pairs={{0,16},{8,24},{16,0},{24,8},{1,17},{9,25},{17,1},{25,9},{2,18},{10... | collective-permute-start | bytes 1695752 | tf_op jit(solution)/shard_map/ppermute | solution.py:451
  72.9 42.9 %collective-permute-start.5 = (f32[4,2,46,384]{3,0,2,1:T(4,128)S(1)}, f32[4,2,46,384]{3,0,2,1:T(4,128)S(1)}, u32[]{:S(2)}, u32[]{:S(2)}) collective-permute-start(f32[4,2,46,384]{3,0,2,1:T(4,128)S(1)} %bitcast.78), channel_id=1, source_target_pairs={{0,24},{8,0},{16,8},{24,16},{1,25},{9,1},{17,9},{25,17},{2,26},{10... | collective-permute-start | bytes 1695752 | tf_op jit(solution)/shard_map/ppermute | solution.py:451
  140.6 1.4 copy-start
  142.0 82.8 %all-to-all-start.1 = ((f32[32,48,384]{2,1,0:T(8,128)}), f32[32,48,384]{2,1,0:T(8,128)}, u32[]{:S(2)}, u32[]{:S(2)}) async-start(f32[32,48,384]{2,1,0:T(8,128)} %bitcast.67), calls=%async_computation.1 | async-start | bytes 4718592 | tf_op jit(solution)/shard_map/all_to_all | solution.py:469
  155.3 31.1 %collective-permute-start.6 = (f32[4,2,46,384]{3,0,2,1:T(4,128)S(1)}, f32[4,2,46,384]{3,0,2,1:T(4,128)S(1)}, u32[]{:S(2)}, u32[]{:S(2)}) collective-permute-start(f32[4,2,46,384]{3,0,2,1:T(4,128)S(1)} %bitcast.84), channel_id=1, source_target_pairs={{0,8},{8,16},{16,24},{24,0},{1,9},{9,17},{17,25},{25,1},{2,10},{10... | collective-permute-start | bytes 1695752 | tf_op jit(solution)/shard_map/ppermute | solution.py:451
  155.5 32.5 %collective-permute-start.7 = (f32[4,2,46,384]{3,0,2,1:T(4,128)S(1)}, f32[4,2,46,384]{3,0,2,1:T(4,128)S(1)}, u32[]{:S(2)}, u32[]{:S(2)}) collective-permute-start(f32[4,2,46,384]{3,0,2,1:T(4,128)S(1)} %bitcast.82), channel_id=1, source_target_pairs={{0,16},{8,24},{16,0},{24,8},{1,17},{9,25},{17,1},{25,9},{2,18},{10... | collective-permute-start | bytes 1695752 | tf_op jit(solution)/shard_map/ppermute | solution.py:451
  157.2 42.8 %collective-permute-start.8 = (f32[4,2,46,384]{3,0,2,1:T(4,128)S(1)}, f32[4,2,46,384]{3,0,2,1:T(4,128)S(1)}, u32[]{:S(2)}, u32[]{:S(2)}) collective-permute-start(f32[4,2,46,384]{3,0,2,1:T(4,128)S(1)} %bitcast.79), channel_id=1, source_target_pairs={{0,24},{8,0},{16,8},{24,16},{1,25},{9,1},{17,9},{25,17},{2,26},{10... | collective-permute-start | bytes 1695752 | tf_op jit(solution)/shard_map/ppermute | solution.py:451
  224.8 81.1 %all-to-all-start.2 = ((f32[32,48,384]{2,1,0:T(8,128)}), f32[32,48,384]{2,1,0:T(8,128)S(1)}, u32[]{:S(2)}, u32[]{:S(2)}) async-start(f32[32,48,384]{2,1,0:T(8,128)} %bitcast.66), calls=%async_computation.2 | async-start | bytes 4718592 | tf_op jit(solution)/shard_map/all_to_all | solution.py:469
  238.0 31.3 %collective-permute-start.9 = (f32[4,2,46,384]{3,0,2,1:T(4,128)S(1)}, f32[4,2,46,384]{3,0,2,1:T(4,128)S(1)}, u32[]{:S(2)}, u32[]{:S(2)}) collective-permute-start(f32[4,2,46,384]{3,0,2,1:T(4,128)S(1)} %bitcast.85), channel_id=1, source_target_pairs={{0,8},{8,16},{16,24},{24,0},{1,9},{9,17},{17,25},{25,1},{2,10},{10... | collective-permute-start | bytes 1695752 | tf_op jit(solution)/shard_map/ppermute | solution.py:451
  238.3 32.6 %collective-permute-start.10 = (f32[4,2,46,384]{3,0,2,1:T(4,128)S(1)}, f32[4,2,46,384]{3,0,2,1:T(4,128)S(1)}, u32[]{:S(2)}, u32[]{:S(2)}) collective-permute-start(f32[4,2,46,384]{3,0,2,1:T(4,128)S(1)} %bitcast.80), channel_id=1, source_target_pairs={{0,16},{8,24},{16,0},{24,8},{1,17},{9,25},{17,1},{25,9},{2,18},{10... | collective-permute-start | bytes 1695752 | tf_op jit(solution)/shard_map/ppermute | solution.py:451
  239.9 42.9 %collective-permute-start.11 = (f32[4,2,46,384]{3,0,2,1:T(4,128)S(1)}, f32[4,2,46,384]{3,0,2,1:T(4,128)S(1)}, u32[]{:S(2)}, u32[]{:S(2)}) collective-permute-start(f32[4,2,46,384]{3,0,2,1:T(4,128)S(1)} %bitcast.77), channel_id=1, source_target_pairs={{0,24},{8,0},{16,8},{24,16},{1,25},{9,1},{17,9},{25,17},{2,26},{10... | collective-permute-start | bytes 1695752 | tf_op jit(solution)/shard_map/ppermute | solution.py:451
  305.9 1.5 copy-start.1
  307.4 66.5 %all-to-all-start.3 = ((f32[32,48,384]{2,1,0:T(8,128)}), f32[32,48,384]{2,1,0:T(8,128)}, u32[]{:S(2)}, u32[]{:S(2)}) async-start(f32[32,48,384]{2,1,0:T(8,128)} %bitcast.69), calls=%async_computation.3 | async-start | bytes 4718592 | tf_op jit(solution)/shard_map/all_to_all | solution.py:469

commit v2 on v1

--- a/solution.py
+++ b/solution.py
@@ -19,7 +19,7 @@
 SMALL = 2.0**-64
 BIG = 2.0**32
 PAD = 8
-VMEM_LIMIT = 60 * 1024 * 1024
+VMEM_LIMIT = 67_000_000
 
 
 def round_up(value, multiple):
@@ -155,13 +155,51 @@
     )(step, inverse, order_cols, value, scale, cos_rows)
 
 
-def gradient_kernel(slots, me_ref, *refs):
-    blocks = refs[:-8]
-    target_ref, high_ref, low_ref, band_ref, out_ref, sums_ref, grads_ref, lat_ref = refs[-8:]
-    groups = len(blocks)
+def cut_kernel(bounds, _, *refs):
+    count = len(refs) // (1 + len(bounds))
+    for index, source in enumerate(refs[:count]):
+        slots = source.shape[0]
+        for cut, (first, last) in enumerate(bounds):
+            rows = min(last, slots) - first
+            for part in range(2):
+                refs[count + cut * count + index][part, :rows] = source[first : first + rows, part, :]
+
+
+def cut_pieces(members, channels, bounds):
+    local, _, _, slots, degrees = members.shape
+    count = channels.shape[0]
+    source = members.transpose(0, 1, 3, 2, 4)
+
+    def in_spec(piece):
+        return pl.BlockSpec((None, None, slots, 2, degrees), lambda e, picked: (e, picked[piece], 0, 0, 0))
+
+    shapes = [(2, last - first, degrees) for first, last in bounds for _ in range(count)]
+    outs = pl.pallas_call(
+        functools.partial(cut_kernel, bounds),
+        name="cut_pieces",
+        out_shape=[jax.ShapeDtypeStruct((local, *shape), jnp.float32) for shape in shapes],
+        grid_spec=pltpu.PrefetchScalarGridSpec(
+            num_scalar_prefetch=1,
+            grid=(local,),
+            in_specs=[in_spec(piece) for piece in range(count)],
+            out_specs=[pl.BlockSpec((None, *shape), lambda e, _: (e, 0, 0, 0)) for shape in shapes],
+        ),
+        compiler_params=pltpu.CompilerParams(vmem_limit_bytes=VMEM_LIMIT),
+        cost_estimate=pl.CostEstimate(
+            flops=0, transcendentals=0, bytes_accessed=16 * count * local * slots * degrees
+        ),
+    )(channels, *[source] * count)
+    return [outs[cut * count : (cut + 1) * count] for cut in range(len(bounds))]
+
+
+def gradient_kernel(slots, groups, table_steps, me_ref, *refs):
+    blocks = refs[:groups]
+    target_ref, band_ref = refs[groups : groups + 2]
+    table_refs = refs[groups + 2 : -4]
+    out_ref, sums_ref, grads_ref, lat_ref = refs[-4:]
     local = blocks[0].shape[0]
     degrees = target_ref.shape[2]
-    width = high_ref.shape[2]
+    width = band_ref.shape[1]
     spaces = out_ref.shape[1]
     width_out = out_ref.shape[3]
     count = groups * local
@@ -225,19 +263,29 @@
 
     lax.fori_loop(0, degrees // 128, lane_tile, 0)
 
-    def transform(slot, _):
-        start = pl.multiple_of(slot * pitch, 8)
-        grad = jnp.concatenate(
-            [grads_ref[tile, pl.ds(start, rows), :] for tile in range(degrees // 128)], axis=1
-        )
-        high, low = split(grad)
-        both = dot(jnp.concatenate([high, low], axis=0), high_ref[slot])
-        lat = both[:rows] + both[rows:] + dot(high, low_ref[slot])
-        for tile in range(width // 128):
-            lat_ref[tile, pl.ds(start, rows), :] = lat[:, tile * 128 : tile * 128 + 128]
-        return 0
-
-    lax.fori_loop(0, 8, transform, 0, unroll=2)
+    def transform(high_ref, low_ref):
+        def one(slot, _):
+            start = pl.multiple_of(slot * pitch, 8)
+            grad = jnp.concatenate(
+                [grads_ref[tile, pl.ds(start, rows), :] for tile in range(degrees // 128)], axis=1
+            )
+            high, low = split(grad)
+            both = dot(jnp.concatenate([high, low], axis=0), high_ref[slot])
+            lat = both[:rows] + both[rows:] + dot(high, low_ref[slot])
+            for tile in range(width // 128):
+                lat_ref[tile, pl.ds(start, rows), :] = lat[:, tile * 128 : tile * 128 + 128]
+            return 0
+
+        lax.fori_loop(0, 8, one, 0, unroll=8 if len(table_steps) == 1 else 4)
+
+    if len(table_steps) == 1:
+        transform(*table_refs)
+    else:
+        first = 0
+        for index, steps in enumerate(table_steps):
+            here = (pl.program_id(0) >= first) & (pl.program_id(0) < first + steps)
+            pl.when(here)(functools.partial(transform, *table_refs[2 * index : 2 * index + 2]))
+            first += steps
 
     band = band_ref[...]
 
@@ -280,20 +328,27 @@
     lax.fori_loop(0, groups, scatter, 0)
 
 
-def lat_payload(me, parts, targets, channel, high, low, spaces):
-    local, _, slots, degrees = parts[0].shape
+def lat_payload(me, slots, parts, targets, channel, first_step, tables, spaces):
+    local, _, _, degrees = parts[0].shape
     groups = len(parts)
-    padded, _, width = high.shape
+    width = tables[0][0].shape[2]
+    steps = [high.shape[0] // 8 for high, _ in tables]
+    padded = 8 * sum(steps)
     per = 2 * local
     lanes_of = width // spaces
     width_out = round_up(per * lanes_of, 128)
     count = groups * local
     band = jnp.broadcast_to((jnp.arange(width, dtype=jnp.int32) // lanes_of)[None], (8, width))
     part_spec = pl.BlockSpec((local, 2, 8, degrees), lambda g, *_: (0, 0, g, 0))
-    table_spec = pl.BlockSpec((8, degrees, width), lambda g, *_: (g, 0, 0))
+    table_specs = []
+    before = 0
+    for size in steps:
+        index = lambda g, *_, size=size, before=before: (jnp.clip(g - before, 0, size - 1), 0, 0)
+        table_specs += [pl.BlockSpec((8, degrees, width), index)] * 2
+        before += size
     pairs = count * (count + 1) // 2
     return pl.pallas_call(
-        functools.partial(gradient_kernel, slots),
+        functools.partial(gradient_kernel, slots, groups, tuple(steps)),
         name="loss_gradient",
         out_shape=jax.ShapeDtypeStruct((groups, spaces, padded, width_out), jnp.float32),
         grid_spec=pltpu.PrefetchScalarGridSpec(
@@ -301,11 +356,10 @@
             grid=(padded // 8,),
             in_specs=[part_spec] * groups
             + [
-                pl.BlockSpec((None, 2, 8, degrees), lambda g, *_: (channel, 0, g, 0)),
-                table_spec,
-                table_spec,
+                pl.BlockSpec((None, 2, 8, degrees), lambda g, *_: (channel, 0, g + first_step, 0)),
                 pl.BlockSpec((8, width), lambda g, *_: (0, 0)),
-            ],
+            ]
+            + table_specs,
             out_specs=pl.BlockSpec((groups, spaces, 8, width_out), lambda g, *_: (0, 0, g, 0)),
             scratch_shapes=[
                 pltpu.VMEM((2 * count, 8, 128), jnp.float32),
@@ -319,32 +373,35 @@
             transcendentals=pairs * padded * degrees,
             bytes_accessed=4 * padded * degrees * width + 16 * count * padded * degrees,
         ),
-    )(me, *parts, targets, high, low, band)
-
-
-def longitude_kernel(got_ref, high_ref, low_ref, out_ref):
+    )(me, *parts, targets, band, *[array for pair in tables for array in pair])
+
+
+def longitude_kernel(count, *refs):
+    out_ref = refs[-1]
     half = out_ref.shape[0]
-    value = got_ref[...].T
-    both = jnp.concatenate([value[:half], value[half : 2 * half]], axis=1)
-    high, low = split(both)
-    out_ref[...] = (
-        dot(high, high_ref[...]) + dot(low, high_ref[...]) + dot(high, low_ref[...])
-    )
-
-
-def to_longitudes(received, high, low, half):
-    groups, depth, width = received.shape
-    whole = lambda shape: pl.BlockSpec(shape, lambda g: (0, 0))
+    total = None
+    for index in range(count):
+        value = refs[index][...].T
+        both = jnp.concatenate([value[:half], value[half : 2 * half]], axis=1)
+        high, low = split(both)
+        basis_high, basis_low = refs[count + 2 * index][...], refs[count + 2 * index + 1][...]
+        part = dot(high, basis_high) + dot(low, basis_high) + dot(high, basis_low)
+        total = part if total is None else total + part
+    out_ref[...] = total
+
+
+def to_longitudes(received, bases, half):
+    groups, _, width = received[0].shape
+    whole = lambda array: pl.BlockSpec(array.shape, lambda g: (0, 0))
+    flat = [array for pair in bases for array in pair]
+    depth = sum(array.shape[1] for array in received)
     return pl.pallas_call(
-        longitude_kernel,
+        functools.partial(longitude_kernel, len(received)),
         name="longitudes",
         out_shape=jax.ShapeDtypeStruct((groups, half, NLON), jnp.float32),
         grid=(groups,),
-        in_specs=[
-            pl.BlockSpec((None, depth, width), lambda g: (g, 0, 0)),
-            whole(high.shape),
-            whole(low.shape),
-        ],
+        in_specs=[pl.BlockSpec((None, *array.shape[1:]), lambda g: (g, 0, 0)) for array in received]
+        + [whole(array) for array in flat],
         out_specs=pl.BlockSpec((None, half, NLON), lambda g: (g, 0, 0)),
         compiler_params=pltpu.CompilerParams(vmem_limit_bytes=VMEM_LIMIT),
         cost_estimate=pl.CostEstimate(
@@ -352,57 +409,85 @@
             transcendentals=0,
             bytes_accessed=4 * groups * (depth * width + half * NLON),
         ),
-    )(received, high, low)
-
-
-def merge_kernel(lats, *refs):
-    ins, out_ref, wide_ref = refs[:-2], refs[-2], refs[-1]
-    chunks = len(ins)
-    groups = ins[0].shape[0]
+    )(*received, *flat)
+
+
+def merge_kernel(lats, lanes_of, got_ref, high_ref, low_ref, *refs):
+    ins, (out_ref, turned_ref, wide_ref) = refs[:-3], refs[-3:]
+    groups, _, _ = got_ref.shape
+    chunks = len(ins) + 1
     channels = groups * chunks
-    padded = ins[0].shape[1]
+    local = pl.num_programs(0)
+    spread = round_up(lanes_of, 8)
     pitch = channels + PAD
-    for group in range(groups):
-        for chunk in range(chunks):
-            channel = group * chunks + chunk
-            for first in range(0, padded, 8):
-                for lane in range(0, NLON, 128):
-                    size = min(128, NLON - lane)
-                    value = ins[chunk][group, first : first + 8, lane : lane + size]
-                    if size < 128:
-                        value = jnp.concatenate([value, jnp.zeros((8, 128 - size), jnp.float32)], axis=1)
-                    wide_ref[lane // 128, pl.ds(first * pitch + channel, 8, pitch), :] = value
+    member = pl.program_id(0)
+
+    @pl.when(member == 0)
+    def _():
+        for group in range(groups):
+            turned = got_ref[group].T
+            for piece in range(turned_ref.shape[1] // spread):
+                turned_ref[group, piece * spread : piece * spread + lanes_of, :] = turned[
+                    piece * lanes_of : (piece + 1) * lanes_of
+                ]
+
+    def part(group, side):
+        start = pl.multiple_of((side * local + member) * spread, 8)
+        return turned_ref[group, pl.ds(start, lanes_of), :]
+
+    rows = [jnp.concatenate([part(group, 0), part(group, 1)], axis=1) for group in range(groups)]
+    high, low = split(jnp.concatenate(rows, axis=0))
+    last = dot(high, high_ref[...]) + dot(low, high_ref[...]) + dot(high, low_ref[...])
+
+    def place(value, channel, first, lane):
+        rows, size = value.shape
+        if size < 128:
+            value = jnp.concatenate([value, jnp.zeros((rows, 128 - size), jnp.float32)], axis=1)
+        wide_ref[lane // 128, pl.ds(first * pitch + channel, rows, pitch), :] = value
+
     for lane in range(0, NLON, 128):
         size = min(128, NLON - lane)
+        for group in range(groups):
+            for first in range(0, lanes_of, 8):
+                rows = min(8, lanes_of - first)
+                for chunk in range(chunks - 1):
+                    value = ins[chunk][group, pl.ds(first, rows), lane : lane + size]
+                    place(value, group * chunks + chunk, first, lane)
+                value = last[group * lanes_of + first :, lane : lane + size][:rows]
+                place(value, group * chunks + chunks - 1, first, lane)
         for lat in range(lats):
             out_ref[lat * channels : (lat + 1) * channels, lane : lane + size] = wide_ref[
                 lane // 128, lat * pitch : lat * pitch + channels, :size
             ]
 
 
-def merge(parts, local, lats, lanes_of):
-    groups = parts[0].shape[0]
-    channels = groups * len(parts)
-    padded = round_up(lanes_of, 8)
-    parts = [
-        part if padded == lanes_of else jnp.pad(
-            part.reshape(groups, local, lanes_of, NLON), ((0, 0), (0, 0), (0, padded - lanes_of), (0, 0))
-        ).reshape(groups, local * padded, NLON)
-        for part in parts
-    ]
+def merge(received, high, low, parts, local, lats, lanes_of):
+    groups, depth, _ = received.shape
+    channels = groups * (len(parts) + 1)
+    parts = [part.reshape(groups, local, lanes_of, NLON) for part in parts]
     out = pl.pallas_call(
-        functools.partial(merge_kernel, lats),
+        functools.partial(merge_kernel, lats, lanes_of),
         name="merge_channels",
         out_shape=jax.ShapeDtypeStruct((local, lats * channels, NLON), jnp.float32),
         grid=(local,),
-        in_specs=[pl.BlockSpec((groups, padded, NLON), lambda e: (0, e, 0))] * len(parts),
+        in_specs=[
+            pl.BlockSpec(received.shape, lambda e: (0, 0, 0)),
+            pl.BlockSpec(high.shape, lambda e: (0, 0)),
+            pl.BlockSpec(low.shape, lambda e: (0, 0)),
+        ]
+        + [pl.BlockSpec((groups, None, lanes_of, NLON), lambda e: (0, e, 0, 0))] * len(parts),
         out_specs=pl.BlockSpec((None, lats * channels, NLON), lambda e: (e, 0, 0)),
-        scratch_shapes=[pltpu.VMEM((pl.cdiv(NLON, 128), padded * (channels + PAD), 128), jnp.float32)],
+        scratch_shapes=[
+            pltpu.VMEM((groups, 2 * local * round_up(lanes_of, 8), depth), jnp.float32),
+            pltpu.VMEM((pl.cdiv(NLON, 128), lanes_of * (channels + PAD), 128), jnp.float32),
+        ],
         compiler_params=pltpu.CompilerParams(vmem_limit_bytes=VMEM_LIMIT),
         cost_estimate=pl.CostEstimate(
-            flops=0, transcendentals=0, bytes_accessed=8 * local * lats * channels * NLON
-        ),
-    )(*parts)
+            flops=6 * local * groups * lanes_of * 2 * depth * NLON,
+            transcendentals=0,
+            bytes_accessed=8 * local * lats * channels * NLON,
+        ),
+    )(received, high, low, *parts)
     return out.reshape(local, lats, channels, NLON).transpose(0, 2, 1, 3)
 
 
@@ -439,12 +524,9 @@
     lat_index = column // lanes_of * lats + inner
     valid = (inner < lats) & (lat_index < NLAT)
 
-    def pieces(source, chunk):
-        result = []
-        for step in range(groups):
-            channel = lax.rem(me + step, groups) * chunks + chunk
-            result.append(lax.dynamic_index_in_dim(source, channel, 1, keepdims=False))
-        return result
+    def pieces(source, chunk, bounds):
+        picked = lax.rem(me + jnp.arange(groups, dtype=jnp.int32), groups) * chunks + chunk
+        return cut_pieces(source, picked.astype(jnp.int32), bounds)
 
     def exchange(cut):
         return [cut[0]] + [
@@ -452,24 +534,43 @@
             for step in range(1, groups)
         ]
 
-    high, low = legendre_tables(mine, degrees, jnp.where(valid, lat_index, 0), valid)
-    basis_high, basis_low = longitude_basis(by_device.reshape(-1))
+    lat_rows = jnp.where(valid, lat_index, 0)
+    head = round_up(padded // 2, 8)
+    items = [(0, 0, head), (0, head, padded)] + [(chunk, 0, padded) for chunk in range(1, chunks)]
     index = me.reshape(1).astype(jnp.int32)
+
     arrived = []
-    outputs = []
-    for chunk in range(chunks):
-        source = members
-        if chunk:
-            source, *arrived[chunk - 1] = lax.optimization_barrier((source, *arrived[chunk - 1]))
-        arrived.append(exchange(pieces(source, chunk)))
-    for chunk in range(chunks):
-        parts = arrived[chunk]
-        payload = lat_payload(index, parts, target, chunk, high, low, spaces)
-        blocks = payload.reshape(groups * spaces, padded, payload.shape[3])
+    early = pieces(members, 0, [item[1:] for item in items[:2]])
+    for cut in early:
+        arrived.append(exchange(cut))
+    for number, (chunk, first, last) in enumerate(items[2:], 2):
+        source, *arrived[-1] = lax.optimization_barrier((members, *arrived[-1]))
+        arrived.append(exchange(pieces(source, chunk, [(first, last)])[0]))
+
+    tables = {}
+    received = []
+    for number, (chunk, first, last) in enumerate(items):
+        if number < 2:
+            tables[number] = legendre_tables(mine[first:last], degrees, lat_rows, valid)
+        used = [tables[number]] if number < 2 else [tables[0], tables[1]]
+        count = min(last, slots) - first
+        payload = lat_payload(
+            index, count, arrived[number], target, chunk, first // 8, used, spaces
+        )
+        if number == 0:
+            payload, mine = lax.optimization_barrier((payload, mine))
+        blocks = payload.reshape(groups * spaces, last - first, payload.shape[3])
         moved = lax.all_to_all(blocks, ("member", "space"), 0, 0, tiled=True)
-        moved = moved.reshape(groups, spaces * padded, payload.shape[3])
-        outputs.append(to_longitudes(moved, basis_high, basis_low, local * lanes_of))
-    return merge(outputs, local, lats, lanes_of)
+        received.append(moved.reshape(groups, spaces * (last - first), payload.shape[3]))
+
+    bases = [
+        longitude_basis(by_device[:, first:last].reshape(-1)) for _, first, last in items[:2]
+    ]
+    full = longitude_basis(by_device.reshape(-1))
+    half = local * lanes_of
+    outputs = [to_longitudes(received[:2], bases, half)]
+    outputs += [to_longitudes([got], [full], half) for got in received[2:-1]]
+    return merge(received[-1], *full, outputs, local, lats, lanes_of)
 
 
 def solution(mesh):

time: 390 us -> 409 us (1.049)
  blocking collectives: 0 us -> 36.5 us
  local copies, waits for them, and re-layouts: 32.7 us -> 4.87 us
  Pallas kernels: 149 us -> 171 us
  waiting for transfers between devices: 148 us -> 134 us
  other arithmetic: 8.65 us -> 17.8 us
  starting transfers between devices: 50.9 us -> 43.1 us
    all_to_all x0 -> x1, blocking collectives: none -> 36.5 us  [shards(): moved = lax.all_to_all(blocks, ('member', 'space'), 0, 0, tiled=True)]
    pallas_call x9 -> x13, Pallas kernels: 125 us -> 143 us  [the longest x5 90.8 us: lat_payload(): pl.pallas_call(functools.partial(gradient_kernel, slots, groups, tuple(st...]
    dynamic_slice x20 -> x1, local copies, waits for them, and re-layouts: 16.3 us -> 0.01 us  [shards(): lax.dynamic_index_in_dim(by_device, lax.axis_index('space'), 0, keepdims=...]
    all_to_all x4, waiting for transfers between devices: 27.7 us -> 19.4 us  [shards(): moved = lax.all_to_all(blocks, ('member', 'space'), 0, 0, tiled=True)]
    all_to_all x4, starting transfers between devices: 36.6 us -> 28.4 us  [shards(): moved = lax.all_to_all(blocks, ('member', 'space'), 0, 0, tiled=True)]
    optimization_barrier x9 -> x0, local copies, waits for them, and re-layouts: 7.95 us -> none  [shards(): lax.optimization_barrier((source, *arrived[chunk - 1]))]
    mul x1 -> x3, other arithmetic: 5.2 us -> 10.5 us  [longitude_basis(): cosine = jnp.where(valid, jnp.cos(angle), 0.0) * scale]
    ppermute x12 -> x15, waiting for transfers between devices: 120 us -> 115 us  [exchange(): lax.ppermute(cut[step], 'member', [(i, (i + step) % groups) for i in rang...]
  transfers between devices with their start and end apart: 16 -> 19, of which waited for: 10 -> 10; matrix products, arithmetic and copies ran while one was open for 8% -> 5% of each run, Pallas kernels for 29% -> 32%
where the time goes in v2:
time: 409 us; the launch traced here: 407 us
  Pallas kernels  171 us (42%)
  waiting for transfers between devices  134 us (33%)
  starting transfers between devices  43.1 us (11%)
  blocking collectives  36.5 us (9%)
  other arithmetic  17.8 us (4%)
  local copies, waits for them, and re-layouts  4.87 us (1%)
    ppermute x15, waiting for transfers between devices, exchange(): lax.ppermute(cut[step], 'member', [(i, (i + step) % groups) for i in rang...  115 us
    pallas_call x5, Pallas kernels, lat_payload(): pl.pallas_call(functools.partial(gradient_kernel, slots, groups, tuple(st...  90.8 us
    all_to_all x1, blocking collectives, shards(): moved = lax.all_to_all(blocks, ('member', 'space'), 0, 0, tiled=True)  36.5 us
    all_to_all x4, starting transfers between devices, shards(): moved = lax.all_to_all(blocks, ('member', 'space'), 0, 0, tiled=True)  28.4 us
    pallas_call x2, Pallas kernels, legendre_tables(): pl.pallas_call(table_kernel, name='legendre_table', out_shape=(shape, sha...  27.6 us
    pallas_call x3, Pallas kernels, to_longitudes(): pl.pallas_call(functools.partial(longitude_kernel, len(received)), name='...  21.7 us
    all_to_all x4, waiting for transfers between devices, shards(): moved = lax.all_to_all(blocks, ('member', 'space'), 0, 0, tiled=True)  19.4 us
    pallas_call x4, Pallas kernels, cut_pieces(): pl.pallas_call(functools.partial(cut_kernel, bounds), name='cut_pieces',...  19.3 us
  transfers between devices with their start and end apart: 19, of which 10 were waited for; matrix products, arithmetic and copies ran while one was open for 5% of the time, Pallas kernels for 32%

profile of v2, /device:TPU:0, one launch (start us, length us, event | category | flops | bytes accessed | tf_op | source)
XLA Modules:
  0.0 407.5 jit_solution(856633134298090520)
XLA Ops:
  0.6 4.9 %cut_pieces.4 = (f32[4,2,24,384]{3,2,1,0:T(8,128)}, f32[4,2,24,384]{3,2,1,0:T(8,128)}, f32[4,2,24,384]{3,2,1,0:T(8,128)}, f32[4,2,24,384]{3,2,1,0:T(8,128)}, f32...) custom-call(s32[4]{0:T(128)} %get-tuple-element.107._, ...), custom_call_target="tpu_custom_call" | custom-call | bytes 4521984 | tf_op jit(solution)/shard_map/cut_pieces/pallas_call | solution.py:177
  6.1 2.6 collective-permute-start.13
  8.6 1.4 collective-permute-start.14
  10.8 1.9 copy.5.refs_4_
  12.7 0.7 floor_minimum_fusion.1
  13.4 0.7 maximum_divide_fusion.inv_ref
  14.1 0.7 broadcast_in_dim.73.order_ref
  15.3 13.8 %legendre_table.2 = (bf16[24,384,384]{2,1,0:T(8,128)(2,1)}, bf16[24,384,384]{2,1,0:T(8,128)(2,1)}) custom-call(f32[384]{0:T(512)} %copy-done, f32[384]{0:T(512)} %maximum_divide_fusion.inv_ref, f32[24,128]{1,0:T(8,128)} %broadcast_in_dim.73.order_ref, f32[24,384]{1,0:T(8,128)} %get-tuple-element.98.value_ref, f32[24,384]{1,0:T(8,128)} %get-tuple-element.97.scale_ref, ...), custom_call_target="tpu_custom_call" | custom-call | flops 35389440 | bytes 14155776 | tf_op jit(solution)/shard_map/legendre_table/pallas_call | solution.py:138
  29.2 1.4 collective-permute-start.2
  31.2 12.0 %loss_gradient.5 = f32[4,8,24,384]{3,2,1,0:T(8,128)} custom-call(s32[1]{0:T(128)} %bitcast.me_ref, f32[4,2,24,384]{3,2,1,0:T(8,128)} %get-tuple-element.67.refs_0_, f32[4,2,24,384]{3,2,1,0:T(8,128)} %collective-permute-done.12.refs_1_, f32[4,2,24,384]{3,2,1,0:T(8,128)} %collective-permute-done.13.refs_2_, f32[4,2,24,384]{3,2,1,0:T(8,128)} %collective-permute-done.14.refs_3_, ...), custom_call_target="tpu_custom_call" | custom-call | flops 679477248 | bytes 16515072 | tf_op jit(solution)/shard_map/loss_gradient/pallas_call | solution.py:350
  43.4 0.7 floor_minimum_fusion
  44.1 0.7 broadcast_in_dim.131.order_ref
  44.8 13.8 %legendre_table.3 = (bf16[24,384,384]{2,1,0:T(8,128)(2,1)}, bf16[24,384,384]{2,1,0:T(8,128)(2,1)}) custom-call(f32[384]{0:T(512)} %copy-done, f32[384]{0:T(512)} %maximum_divide_fusion.inv_ref, f32[24,128]{1,0:T(8,128)} %broadcast_in_dim.131.order_ref, f32[24,384]{1,0:T(8,128)} %get-tuple-element.96.value_ref, f32[24,384]{1,0:T(8,128)} %get-tuple-element.95.scale_ref, ...), custom_call_target="tpu_custom_call" | custom-call | flops 35389440 | bytes 14155776 | tf_op jit(solution)/shard_map/legendre_table/pallas_call | solution.py:138
  58.5 11.9 %loss_gradient.7 = f32[4,8,24,384]{3,2,1,0:T(8,128)} custom-call(s32[1]{0:T(128)} %bitcast.me_ref, f32[4,2,24,384]{3,2,1,0:T(8,128)} %get-tuple-element.75.refs_0_, f32[4,2,24,384]{3,2,1,0:T(8,128)} %collective-permute-done.refs_1_, f32[4,2,24,384]{3,2,1,0:T(8,128)} %collective-permute-done.1.refs_2_, f32[4,2,24,384]{3,2,1,0:T(8,128)} %collective-permute-done.2.refs_3_, ...), custom_call_target="tpu_custom_call" | custom-call | flops 679477248 | bytes 16515072 | tf_op jit(solution)/shard_map/loss_gradient/pallas_call | solution.py:350
  70.4 36.5 %all_to_all.25 = f32[32,24,384]{2,1,0:T(8,128)} all-to-all(f32[32,24,384]{2,1,0:T(8,128)} %bitcast.49), channel_id=1, replica_groups=mesh['member'=4,'space'=8] {'member','space'}, dimensions={0} | all-to-all | bytes 2359296 | tf_op jit(solution)/shard_map/all_to_all | solution.py:563
  106.9 3.4 all-to-all-start.1
  110.3 4.8 %cut_pieces.5 = (f32[4,2,48,384]{3,2,1,0:T(8,128)}, f32[4,2,48,384]{3,2,1,0:T(8,128)}, f32[4,2,48,384]{3,2,1,0:T(8,128)}, f32[4,2,48,384]{3,2,1,0:T(8,128)}) custom-call(s32[4]{0:T(128)} %get-tuple-element.108._, f32[4,16,46,2,384]{4,3,2,1,0:T(2,128)} %bitcast.34, f32[4,16,46,2,384]{4,3,2,1,0:T(2,128)} %bitcast.35, f32[4,16,46,2,384]{4,3,2,1,0:T(2,128)} %bitcast.36, ...), custom_call_target="tpu_custom_call" | custom-call | bytes 4521984 | tf_op jit(solution)/shard_map/cut_pieces/pallas_call | solution.py:177
  115.1 1.6 collective-permute-start.4
  116.8 1.3 collective-permute-start.5
  118.1 18.6 %collective-permute-done.3.refs_1_ = f32[4,2,48,384]{3,2,1,0:T(8,128)} collective-permute-done((f32[4,2,48,384]{3,2,1,0:T(8,128)}, f32[4,2,48,384]{3,2,1,0:T(8,128)}, u32[]{:S(2)}, u32[]{:S(2)}) %collective-permute-start.3) | collective-permute-done | bytes 589856 | tf_op jit(solution)/shard_map/ppermute | solution.py:533
  137.3 12.0 %collective-permute-done.5.refs_3_ = f32[4,2,48,384]{3,2,1,0:T(8,128)} collective-permute-done((f32[4,2,48,384]{3,2,1,0:T(8,128)}, f32[4,2,48,384]{3,2,1,0:T(8,128)}, u32[]{:S(2)}, u32[]{:S(2)}) %collective-permute-start.5) | collective-permute-done | bytes 589856 | tf_op jit(solution)/shard_map/ppermute | solution.py:533
  149.3 22.3 %loss_gradient.8 = f32[4,8,48,384]{3,2,1,0:T(8,128)} custom-call(s32[1]{0:T(128)} %bitcast.me_ref, f32[4,2,48,384]{3,2,1,0:T(8,128)} %get-tuple-element.79.refs_0_, f32[4,2,48,384]{3,2,1,0:T(8,128)} %collective-permute-done.3.refs_1_, f32[4,2,48,384]{3,2,1,0:T(8,128)} %collective-permute-done.4.refs_2_, f32[4,2,48,384]{3,2,1,0:T(8,128)} %collective-permute-done.5.refs_3_, ...), custom_call_target="tpu_custom_call" | custom-call | flops 1358954496 | bytes 33030144 | tf_op jit(solution)/shard_map/loss_gradient/pallas_call | solution.py:350
  171.6 5.9 %all-to-all-start.3 = ((f32[32,48,384]{2,1,0:T(8,128)}), f32[32,48,384]{2,1,0:T(8,128)}, u32[]{:S(2)}, u32[]{:S(2)}) async-start(f32[32,48,384]{2,1,0:T(8,128)} %bitcast.48), calls=%async_computation.3 | async-start | bytes 4718592 | tf_op jit(solution)/shard_map/all_to_all | solution.py:563
  178.1 4.8 %cut_pieces.6 = (f32[4,2,48,384]{3,2,1,0:T(8,128)}, f32[4,2,48,384]{3,2,1,0:T(8,128)}, f32[4,2,48,384]{3,2,1,0:T(8,128)}, f32[4,2,48,384]{3,2,1,0:T(8,128)}) custom-call(s32[4]{0:T(128)} %get-tuple-element.109._, f32[4,16,46,2,384]{4,3,2,1,0:T(2,128)} %bitcast.38, f32[4,16,46,2,384]{4,3,2,1,0:T(2,128)} %bitcast.39, f32[4,16,46,2,384]{4,3,2,1,0:T(2,128)} %bitcast.40, ...), custom_call_target="tpu_custom_call" | custom-call | bytes 4521984 | tf_op jit(solution)/shard_map/cut_pieces/pallas_call | solution.py:177
  183.1 1.6 collective-permute-start.7
  184.7 1.4 collective-permute-start.8
  186.1 26.1 %collective-permute-done.6.refs_1_ = f32[4,2,48,384]{3,2,1,0:T(8,128)} collective-permute-done((f32[4,2,48,384]{3,2,1,0:T(8,128)}, f32[4,2,48,384]{3,2,1,0:T(8,128)}, u32[]{:S(2)}, u32[]{:S(2)}) %collective-permute-start.6) | collective-permute-done | bytes 589856 | tf_op jit(solution)/shard_map/ppermute | solution.py:533
  212.2 1.9 collective-permute-done.7.refs_2_
  214.1 12.4 %collective-permute-done.8.refs_3_ = f32[4,2,48,384]{3,2,1,0:T(8,128)} collective-permute-done((f32[4,2,48,384]{3,2,1,0:T(8,128)}, f32[4,2,48,384]{3,2,1,0:T(8,128)}, u32[]{:S(2)}, u32[]{:S(2)}) %collective-permute-start.8) | collective-permute-done | bytes 589856 | tf_op jit(solution)/shard_map/ppermute | solution.py:533
  226.4 22.4 %loss_gradient.9 = f32[4,8,48,384]{3,2,1,0:T(8,128)} custom-call(s32[1]{0:T(128)} %bitcast.me_ref, f32[4,2,48,384]{3,2,1,0:T(8,128)} %get-tuple-element.83.refs_0_, f32[4,2,48,384]{3,2,1,0:T(8,128)} %collective-permute-done.6.refs_1_, f32[4,2,48,384]{3,2,1,0:T(8,128)} %collective-permute-done.7.refs_2_, f32[4,2,48,384]{3,2,1,0:T(8,128)} %collective-permute-done.8.refs_3_, ...), custom_call_target="tpu_custom_call" | custom-call | flops 1358954496 | bytes 33030144 | tf_op jit(solution)/shard_map/loss_gradient/pallas_call | solution.py:350
  248.8 10.2 %all-to-all-start.4 = ((f32[32,48,384]{2,1,0:T(8,128)}), f32[32,48,384]{2,1,0:T(8,128)}, u32[]{:S(2)}, u32[]{:S(2)}) async-start(f32[32,48,384]{2,1,0:T(8,128)} %bitcast.47), calls=%async_computation.4 | async-start | bytes 4718592 | tf_op jit(solution)/shard_map/all_to_all | solution.py:563
  259.0 4.8 %cut_pieces.7 = (f32[4,2,48,384]{3,2,1,0:T(8,128)}, f32[4,2,48,384]{3,2,1,0:T(8,128)}, f32[4,2,48,384]{3,2,1,0:T(8,128)}, f32[4,2,48,384]{3,2,1,0:T(8,128)}) custom-call(s32[4]{0:T(128)} %get-tuple-element.110._, f32[4,16,46,2,384]{4,3,2,1,0:T(2,128)} %bitcast.42, f32[4,16,46,2,384]{4,3,2,1,0:T(2,128)} %bitcast.43, f32[4,16,46,2,384]{4,3,2,1,0:T(2,128)} %bitcast.44, ...), custom_call_target="tpu_custom_call" | custom-call | bytes 4521984 | tf_op jit(solution)/shard_map/cut_pieces/pallas_call | solution.py:177
  263.8 1.7 collective-permute-start.10
  266.0 29.6 %collective-permute-done.10.refs_2_ = f32[4,2,48,384]{3,2,1,0:T(8,128)} collective-permute-done((f32[4,2,48,384]{3,2,1,0:T(8,128)}, f32[4,2,48,384]{3,2,1,0:T(8,128)}, u32[]{:S(2)}, u32[]{:S(2)}) %collective-permute-start.10) | collective-permute-done | bytes 589856 | tf_op jit(solution)/shard_map/ppermute | solution.py:533
  295.6 12.4 %collective-permute-done.11.refs_3_ = f32[4,2,48,384]{3,2,1,0:T(8,128)} collective-permute-done((f32[4,2,48,384]{3,2,1,0:T(8,128)}, f32[4,2,48,384]{3,2,1,0:T(8,128)}, u32[]{:S(2)}, u32[]{:S(2)}) %collective-permute-start.11) | collective-permute-done | bytes 589856 | tf_op jit(solution)/shard_map/ppermute | solution.py:533
  307.9 1.5 collective-permute-done.9.refs_1_
  309.4 22.4 %loss_gradient.6 = f32[4,8,48,384]{3,2,1,0:T(8,128)} custom-call(s32[1]{0:T(128)} %bitcast.me_ref, f32[4,2,48,384]{3,2,1,0:T(8,128)} %get-tuple-element.61.refs_0_, f32[4,2,48,384]{3,2,1,0:T(8,128)} %collective-permute-done.9.refs_1_, f32[4,2,48,384]{3,2,1,0:T(8,128)} %collective-permute-done.10.refs_2_, f32[4,2,48,384]{3,2,1,0:T(8,128)} %collective-permute-done.11.refs_3_, ...), custom_call_target="tpu_custom_call" | custom-call | flops 1358954496 | bytes 33030144 | tf_op jit(solution)/shard_map/loss_gradient/pallas_call | solution.py:350
  331.8 8.9 %all-to-all-start = ((f32[32,48,384]{2,1,0:T(8,128)}), f32[32,48,384]{2,1,0:T(8,128)}, u32[]{:S(2)}, u32[]{:S(2)}) async-start(f32[32,48,384]{2,1,0:T(8,128)} %bitcast.46), calls=%async_computation | async-start | bytes 4718592 | tf_op jit(solution)/shard_map/all_to_all | solution.py:563
  341.1 5.2 %select_multiply_fusion.1 = (f32[384,720]{1,0:T(8,128)S(1)}, f32[384,720]{1,0:T(8,128)S(1)}) fusion(s32[384]{0:T(512)S(1)} %reshape.277, pred[384]{0:T(512)(128)(4,1)S(1)} %broadcast_compare_fusion), kind=kLoop, calls=%fused_computation.16 | loop fusion | flops 3870720 | bytes 2213760 | tf_op jit(solution)/shard_map/mul | solution.py:500
  346.3 1.9 fusion
  348.2 2.6 select_multiply_fusion.3
  350.8 2.6 select_multiply_fusion.5
  353.5 1.7 fusion.1
  355.2 7.9 %longitudes.3 = f32[4,192,720]{2,1,0:T(8,128)} custom-call(f32[4,192,384]{2,1,0:T(8,128)} %bitcast.11.refs_0_, f32[4,192,384]{2,1,0:T(8,128)} %bitcast.53, bf16[384,720]{1,0:T(8,128)(2,1)} %get-tuple-element.92.refs_2_, bf16[384,720]{1,0:T(8,128)(2,1)} %get-tuple-element.91.refs_3_, bf16[384,720]{1,0:T(8,128)(2,1)} %get-tuple-element.113.refs_4_, ...), custom_call_target="tpu_custom_call" | custom-call | flops 2548039680 | bytes 4571136 | tf_op jit(solution)/shard_map/longitudes/pallas_call | solution.py:398
  363.0 6.9 %longitudes.4 = f32[4,192,720]{2,1,0:T(8,128)} custom-call(f32[4,384,384]{2,1,0:T(8,128)} %bitcast.16.refs_0_, bf16[768,720]{1,0:T(8,128)(2,1)} %get-tuple-element.88.refs_1_.high_ref, bf16[768,720]{1,0:T(8,128)(2,1)} %get-tuple-element.87.refs_2_.low_ref), custom_call_target="tpu_custom_call" | custom-call | flops 2548039680 | bytes 4571136 | tf_op jit(solution)/shard_map/longitudes/pallas_call | solution.py:398
  370.0 6.9 %longitudes.5 = f32[4,192,720]{2,1,0:T(8,128)} custom-call(f32[4,384,384]{2,1,0:T(8,128)} %bitcast.19.refs_0_, bf16[768,720]{1,0:T(8,128)(2,1)} %get-tuple-element.88.refs_1_.high_ref, bf16[768,720]{1,0:T(8,128)(2,1)} %get-tuple-element.87.refs_2_.low_ref), custom_call_target="tpu_custom_call" | custom-call | flops 2548039680 | bytes 4571136 | tf_op jit(solution)/shard_map/longitudes/pallas_call | solution.py:398
  376.9 19.4 %all-to-all-done = f32[32,48,384]{2,1,0:T(8,128)} async-done(((f32[32,48,384]{2,1,0:T(8,128)}), f32[32,48,384]{2,1,0:T(8,128)}, u32[]{:S(2)}, u32[]{:S(2)}) %all-to-all-start) | async-done | bytes 2359328 | tf_op jit(solution)/shard_map/all_to_all | solution.py:563
  396.3 11.2 %merge_channels.1 = f32[4,736,720]{2,1,0:T(8,128)} custom-call(f32[4,384,384]{2,1,0:T(8,128)} %bitcast.9.got_ref, bf16[768,720]{1,0:T(8,128)(2,1)} %get-tuple-element.88.refs_1_.high_ref, bf16[768,720]{1,0:T(8,128)(2,1)} %get-tuple-element.87.refs_2_.low_ref, f32[4,4,48,720]{3,2,1,0:T(8,128)} %bitcast.50, f32[4,4,48,720]{3,2,1,0:T(8,128)} %bitcast.51, ...), custom_call_target="tpu_custom_call" | custom-call | flops 2548039680 | bytes 16957440 | tf_op jit(solution)/shard_map/merge_channels/pallas_call | solution.py:468
  (45 shorter events, 5.6 us)
Async XLA Ops:
  0.6 9.8 %copy-start.1 = (s32[368]{0:T(512)S(1)}, s32[368]{0:T(512)}, u32[]{:S(2)}) copy-start(s32[368]{0:T(512)} %param.5) | copy-start | bytes 4420
  5.5 23.6 %collective-permute-start.12 = (f32[4,2,24,384]{3,2,1,0:T(8,128)}, f32[4,2,24,384]{3,2,1,0:T(8,128)}, u32[]{:S(2)}, u32[]{:S(2)}) collective-permute-start(f32[4,2,24,384]{3,2,1,0:T(8,128)} %get-tuple-element.68), channel_id=1, source_target_pairs={{0,8},{8,16},{16,24},{24,0},{1,9},{9,17},{17,25},{25,1},{2,10},{10... | collective-permute-start | bytes 884744 | tf_op jit(solution)/shard_map/ppermute | solution.py:533
  6.1 24.5 %collective-permute-start.13 = (f32[4,2,24,384]{3,2,1,0:T(8,128)}, f32[4,2,24,384]{3,2,1,0:T(8,128)}, u32[]{:S(2)}, u32[]{:S(2)}) collective-permute-start(f32[4,2,24,384]{3,2,1,0:T(8,128)} %get-tuple-element.69), channel_id=1, source_target_pairs={{0,16},{8,24},{16,0},{24,8},{1,17},{9,25},{17,1},{25,9},{2,18},{10... | collective-permute-start | bytes 884744 | tf_op jit(solution)/shard_map/ppermute | solution.py:533
  8.6 22.0 %collective-permute-start.14 = (f32[4,2,24,384]{3,2,1,0:T(8,128)}, f32[4,2,24,384]{3,2,1,0:T(8,128)}, u32[]{:S(2)}, u32[]{:S(2)}) collective-permute-start(f32[4,2,24,384]{3,2,1,0:T(8,128)} %get-tuple-element.70), channel_id=1, source_target_pairs={{0,24},{8,0},{16,8},{24,16},{1,25},{9,1},{17,9},{25,17},{2,26},{10... | collective-permute-start | bytes 884744 | tf_op jit(solution)/shard_map/ppermute | solution.py:533
  10.0 33.4 %collective-permute-start = (f32[4,2,24,384]{3,2,1,0:T(8,128)}, f32[4,2,24,384]{3,2,1,0:T(8,128)}, u32[]{:S(2)}, u32[]{:S(2)}) collective-permute-start(f32[4,2,24,384]{3,2,1,0:T(8,128)} %get-tuple-element.47), channel_id=1, source_target_pairs={{0,8},{8,16},{16,24},{24,0},{1,9},{9,17},{17,25},{25,1},{2,10},{10... | collective-permute-start | bytes 884744 | tf_op jit(solution)/shard_map/ppermute | solution.py:533
  10.0 33.4 %collective-permute-start.1 = (f32[4,2,24,384]{3,2,1,0:T(8,128)}, f32[4,2,24,384]{3,2,1,0:T(8,128)}, u32[]{:S(2)}, u32[]{:S(2)}) collective-permute-start(f32[4,2,24,384]{3,2,1,0:T(8,128)} %get-tuple-element.48), channel_id=1, source_target_pairs={{0,16},{8,24},{16,0},{24,8},{1,17},{9,25},{17,1},{25,9},{2,18},{10... | collective-permute-start | bytes 884744 | tf_op jit(solution)/shard_map/ppermute | solution.py:533
  10.7 4.6 %copy-start = (f32[384]{0:T(512)}, f32[384]{0:T(512)S(1)}, u32[]{:S(2)}) copy-start(f32[384]{0:T(512)S(1)} %maximum_sqrt_fusion.step_ref) | copy-start | bytes 4612
  29.2 14.2 %collective-permute-start.2 = (f32[4,2,24,384]{3,2,1,0:T(8,128)}, f32[4,2,24,384]{3,2,1,0:T(8,128)}, u32[]{:S(2)}, u32[]{:S(2)}) collective-permute-start(f32[4,2,24,384]{3,2,1,0:T(8,128)} %get-tuple-element.49), channel_id=1, source_target_pairs={{0,24},{8,0},{16,8},{24,16},{1,25},{9,1},{17,9},{25,17},{2,26},{10... | collective-permute-start | bytes 884744 | tf_op jit(solution)/shard_map/ppermute | solution.py:533
  106.9 64.7 %all-to-all-start.1 = ((f32[32,24,384]{2,1,0:T(8,128)}), f32[32,24,384]{2,1,0:T(8,128)}, u32[]{:S(2)}, u32[]{:S(2)}) async-start(f32[32,24,384]{2,1,0:T(8,128)} %bitcast.10), calls=%async_computation.1 | async-start | bytes 2359296 | tf_op jit(solution)/shard_map/all_to_all | solution.py:563
  115.1 21.6 %collective-permute-start.3 = (f32[4,2,48,384]{3,2,1,0:T(8,128)}, f32[4,2,48,384]{3,2,1,0:T(8,128)}, u32[]{:S(2)}, u32[]{:S(2)}) collective-permute-start(f32[4,2,48,384]{3,2,1,0:T(8,128)} %get-tuple-element.52), channel_id=1, source_target_pairs={{0,8},{8,16},{16,24},{24,0},{1,9},{9,17},{17,25},{25,1},{2,10},{10... | collective-permute-start | bytes 1769480 | tf_op jit(solution)/shard_map/ppermute | solution.py:533
  115.1 22.2 %collective-permute-start.4 = (f32[4,2,48,384]{3,2,1,0:T(8,128)}, f32[4,2,48,384]{3,2,1,0:T(8,128)}, u32[]{:S(2)}, u32[]{:S(2)}) collective-permute-start(f32[4,2,48,384]{3,2,1,0:T(8,128)} %get-tuple-element.53), channel_id=1, source_target_pairs={{0,16},{8,24},{16,0},{24,8},{1,17},{9,25},{17,1},{25,9},{2,18},{10... | collective-permute-start | bytes 1769480 | tf_op jit(solution)/shard_map/ppermute | solution.py:533
  116.8 32.5 %collective-permute-start.5 = (f32[4,2,48,384]{3,2,1,0:T(8,128)}, f32[4,2,48,384]{3,2,1,0:T(8,128)}, u32[]{:S(2)}, u32[]{:S(2)}) collective-permute-start(f32[4,2,48,384]{3,2,1,0:T(8,128)} %get-tuple-element.54), channel_id=1, source_target_pairs={{0,24},{8,0},{16,8},{24,16},{1,25},{9,1},{17,9},{25,17},{2,26},{10... | collective-permute-start | bytes 1769480 | tf_op jit(solution)/shard_map/ppermute | solution.py:533
  171.6 77.2 %all-to-all-start.3 = ((f32[32,48,384]{2,1,0:T(8,128)}), f32[32,48,384]{2,1,0:T(8,128)}, u32[]{:S(2)}, u32[]{:S(2)}) async-start(f32[32,48,384]{2,1,0:T(8,128)} %bitcast.48), calls=%async_computation.3 | async-start | bytes 4718592 | tf_op jit(solution)/shard_map/all_to_all | solution.py:563
  182.9 29.3 %collective-permute-start.6 = (f32[4,2,48,384]{3,2,1,0:T(8,128)}, f32[4,2,48,384]{3,2,1,0:T(8,128)}, u32[]{:S(2)}, u32[]{:S(2)}) collective-permute-start(f32[4,2,48,384]{3,2,1,0:T(8,128)} %get-tuple-element.57), channel_id=1, source_target_pairs={{0,8},{8,16},{16,24},{24,0},{1,9},{9,17},{17,25},{25,1},{2,10},{10... | collective-permute-start | bytes 1769480 | tf_op jit(solution)/shard_map/ppermute | solution.py:533
  183.1 31.0 %collective-permute-start.7 = (f32[4,2,48,384]{3,2,1,0:T(8,128)}, f32[4,2,48,384]{3,2,1,0:T(8,128)}, u32[]{:S(2)}, u32[]{:S(2)}) collective-permute-start(f32[4,2,48,384]{3,2,1,0:T(8,128)} %get-tuple-element.58), channel_id=1, source_target_pairs={{0,16},{8,24},{16,0},{24,8},{1,17},{9,25},{17,1},{25,9},{2,18},{10... | collective-permute-start | bytes 1769480 | tf_op jit(solution)/shard_map/ppermute | solution.py:533
  184.7 41.7 %collective-permute-start.8 = (f32[4,2,48,384]{3,2,1,0:T(8,128)}, f32[4,2,48,384]{3,2,1,0:T(8,128)}, u32[]{:S(2)}, u32[]{:S(2)}) collective-permute-start(f32[4,2,48,384]{3,2,1,0:T(8,128)} %get-tuple-element.59), channel_id=1, source_target_pairs={{0,24},{8,0},{16,8},{24,16},{1,25},{9,1},{17,9},{25,17},{2,26},{10... | collective-permute-start | bytes 1769480 | tf_op jit(solution)/shard_map/ppermute | solution.py:533
  248.8 83.0 %all-to-all-start.4 = ((f32[32,48,384]{2,1,0:T(8,128)}), f32[32,48,384]{2,1,0:T(8,128)}, u32[]{:S(2)}, u32[]{:S(2)}) async-start(f32[32,48,384]{2,1,0:T(8,128)} %bitcast.47), calls=%async_computation.4 | async-start | bytes 4718592 | tf_op jit(solution)/shard_map/all_to_all | solution.py:563
  263.8 31.8 %collective-permute-start.10 = (f32[4,2,48,384]{3,2,1,0:T(8,128)}, f32[4,2,48,384]{3,2,1,0:T(8,128)}, u32[]{:S(2)}, u32[]{:S(2)}) collective-permute-start(f32[4,2,48,384]{3,2,1,0:T(8,128)} %get-tuple-element.63), channel_id=1, source_target_pairs={{0,16},{8,24},{16,0},{24,8},{1,17},{9,25},{17,1},{25,9},{2,18},{10... | collective-permute-start | bytes 1769480 | tf_op jit(solution)/shard_map/ppermute | solution.py:533
  265.5 42.4 %collective-permute-start.11 = (f32[4,2,48,384]{3,2,1,0:T(8,128)}, f32[4,2,48,384]{3,2,1,0:T(8,128)}, u32[]{:S(2)}, u32[]{:S(2)}) collective-permute-start(f32[4,2,48,384]{3,2,1,0:T(8,128)} %get-tuple-element.64), channel_id=1, source_target_pairs={{0,24},{8,0},{16,8},{24,16},{1,25},{9,1},{17,9},{25,17},{2,26},{10... | collective-permute-start | bytes 1769480 | tf_op jit(solution)/shard_map/ppermute | solution.py:533
  265.5 43.9 %collective-permute-start.9 = (f32[4,2,48,384]{3,2,1,0:T(8,128)}, f32[4,2,48,384]{3,2,1,0:T(8,128)}, u32[]{:S(2)}, u32[]{:S(2)}) collective-permute-start(f32[4,2,48,384]{3,2,1,0:T(8,128)} %get-tuple-element.62), channel_id=1, source_target_pairs={{0,8},{8,16},{16,24},{24,0},{1,9},{9,17},{17,25},{25,1},{2,10},{10... | collective-permute-start | bytes 1769480 | tf_op jit(solution)/shard_map/ppermute | solution.py:533
  331.8 64.5 %all-to-all-start = ((f32[32,48,384]{2,1,0:T(8,128)}), f32[32,48,384]{2,1,0:T(8,128)}, u32[]{:S(2)}, u32[]{:S(2)}) async-start(f32[32,48,384]{2,1,0:T(8,128)} %bitcast.46), calls=%async_computation | async-start | bytes 4718592 | tf_op jit(solution)/shard_map/all_to_all | solution.py:563

commit v3 on v2

--- a/solution.py
+++ b/solution.py
@@ -65,9 +65,7 @@
             degree = index * 8 + sub
             deg_f = degree.astype(jnp.float32)
             gap_now = deg_f * deg_f - order_sq
-            safe = jnp.maximum(gap_now, 1.0)
-            root_now = lax.rsqrt(safe)
-            root_now = root_now * (1.5 - 0.5 * safe * root_now * root_now)
+            root_now = lax.rsqrt(jnp.maximum(gap_now, 1.0))
             coef_a = step_ref[degree] * root_now
             coef_b = jnp.maximum(gap, 0.0) * root * inv_ref[degree]
             current = wide(coef_a) * (cosine * prev - wide(coef_b) * prev2)
@@ -105,7 +103,7 @@
     lax.fori_loop(0, group, convert, 0)
 
 
-def legendre_tables(orders, degrees, lats, valid):
+def table_inputs(orders, degrees, lats, valid):
     count = orders.shape[0]
     width = lats.shape[0]
     span = float(NLAT - 1)
@@ -129,9 +127,15 @@
     square = jnp.arange(degrees, dtype=jnp.float32) ** 2
     step = jnp.sqrt(jnp.maximum(4.0 * square - 1.0, 1.0))
     inverse = 1.0 / jnp.concatenate([jnp.ones((1,), jnp.float32), step[:-1]])
-    group = 8
     order_cols = jnp.broadcast_to(order_f[:, None], (count, 128))
     cos_rows = jnp.broadcast_to(cosines[None, :], (8, width))
+    return step, inverse, order_cols, value, scale, cos_rows
+
+
+def legendre_tables(orders, degrees, lats, valid):
+    step, inverse, order_cols, value, scale, cos_rows = table_inputs(orders, degrees, lats, valid)
+    count, width = value.shape
+    group = 8
     rows = lambda cols: pl.BlockSpec((group, cols), lambda g, *_: (g, 0))
     out = pl.BlockSpec((group, degrees, width), lambda g, *_: (g, 0, 0))
     shape = jax.ShapeDtypeStruct((count, degrees, width), jnp.bfloat16)
@@ -251,7 +255,7 @@
                         sums = [sums[0] - pull[0], sums[1] - pull[1]]
                 for r in range(2):
                     sums_ref[2 * other + r] = sums[r]
-            goal = (target_ref[0, :, lanes], target_ref[1, :, lanes])
+            goal = (target_ref[:, 0, lanes], target_ref[:, 1, lanes])
             owner = lax.rem(me_ref[0] + (groups - group), groups)
             for e in range(local):
                 pull = force(mine[e], goal)
@@ -328,11 +332,28 @@
     lax.fori_loop(0, groups, scatter, 0)
 
 
-def lat_payload(me, slots, parts, targets, channel, first_step, tables, spaces):
+def fused_kernel(slots, groups, me_ref, step_ref, inv_ref, *refs):
+    blocks, rest = refs[:groups], refs[groups:]
+    target_ref, band_ref, order_ref, value_ref, scale_ref, cos_ref = rest[:6]
+    out_ref, high_ref, low_ref, sums_ref, grads_ref, lat_ref, rows_ref = rest[6:]
+    table_kernel(
+        step_ref, inv_ref, order_ref, value_ref, scale_ref, cos_ref, high_ref, low_ref, rows_ref
+    )
+    gradient_kernel(
+        slots, groups, (1,), me_ref, *blocks, target_ref, band_ref, high_ref, low_ref,
+        out_ref, sums_ref, grads_ref, lat_ref,
+    )
+
+
+def lat_payload(me, slots, parts, targets, channel, first_step, tables, spaces, build=None):
     local, _, _, degrees = parts[0].shape
     groups = len(parts)
-    width = tables[0][0].shape[2]
-    steps = [high.shape[0] // 8 for high, _ in tables]
+    if build is None:
+        width = tables[0][0].shape[2]
+        steps = [high.shape[0] // 8 for high, _ in tables]
+    else:
+        count_rows, width = build[3].shape
+        steps = [count_rows // 8]
     padded = 8 * sum(steps)
     per = 2 * local
     lanes_of = width // spaces
@@ -340,32 +361,46 @@
     count = groups * local
     band = jnp.broadcast_to((jnp.arange(width, dtype=jnp.int32) // lanes_of)[None], (8, width))
     part_spec = pl.BlockSpec((local, 2, 8, degrees), lambda g, *_: (0, 0, g, 0))
-    table_specs = []
-    before = 0
-    for size in steps:
-        index = lambda g, *_, size=size, before=before: (jnp.clip(g - before, 0, size - 1), 0, 0)
-        table_specs += [pl.BlockSpec((8, degrees, width), index)] * 2
-        before += size
+    in_specs = [part_spec] * groups + [
+        pl.BlockSpec((None, 8, 2, degrees), lambda g, *_: (channel, g + first_step, 0, 0)),
+        pl.BlockSpec((8, width), lambda g, *_: (0, 0)),
+    ]
+    out_shape = [jax.ShapeDtypeStruct((groups, spaces, padded, width_out), jnp.float32)]
+    out_specs = [pl.BlockSpec((groups, spaces, 8, width_out), lambda g, *_: (0, 0, g, 0))]
+    scratch = [
+        pltpu.VMEM((2 * count, 8, 128), jnp.float32),
+        pltpu.VMEM((degrees // 128, 8 * (2 * count + PAD), 128), jnp.float32),
+        pltpu.VMEM((width // 128, 8 * (2 * count + PAD), 128), jnp.float32),
+    ]
+    scalars = (me,)
+    if build is None:
+        kernel = functools.partial(gradient_kernel, slots, groups, tuple(steps))
+        before = 0
+        for size in steps:
+            index = lambda g, *_, size=size, before=before: (jnp.clip(g - before, 0, size - 1), 0, 0)
+            in_specs += [pl.BlockSpec((8, degrees, width), index)] * 2
+            before += size
+        extra = [array for pair in tables for array in pair]
+    else:
+        kernel = functools.partial(fused_kernel, slots, groups)
+        scalars += build[:2]
+        extra = list(build[2:])
+        rows = lambda cols: pl.BlockSpec((8, cols), lambda g, *_: (g, 0))
+        in_specs += [rows(128), rows(width), rows(width), pl.BlockSpec((8, width), lambda g, *_: (0, 0))]
+        out_shape += [jax.ShapeDtypeStruct((padded, degrees, width), jnp.bfloat16)] * 2
+        out_specs += [pl.BlockSpec((8, degrees, width), lambda g, *_: (g, 0, 0))] * 2
+        scratch.append(pltpu.VMEM((width // 128, 8 * (degrees + PAD), 128), jnp.float32))
     pairs = count * (count + 1) // 2
-    return pl.pallas_call(
-        functools.partial(gradient_kernel, slots, groups, tuple(steps)),
+    outs = pl.pallas_call(
+        kernel,
         name="loss_gradient",
-        out_shape=jax.ShapeDtypeStruct((groups, spaces, padded, width_out), jnp.float32),
+        out_shape=out_shape,
         grid_spec=pltpu.PrefetchScalarGridSpec(
-            num_scalar_prefetch=1,
+            num_scalar_prefetch=len(scalars),
             grid=(padded // 8,),
-            in_specs=[part_spec] * groups
-            + [
-                pl.BlockSpec((None, 2, 8, degrees), lambda g, *_: (channel, 0, g + first_step, 0)),
-                pl.BlockSpec((8, width), lambda g, *_: (0, 0)),
-            ]
-            + table_specs,
-            out_specs=pl.BlockSpec((groups, spaces, 8, width_out), lambda g, *_: (0, 0, g, 0)),
-            scratch_shapes=[
-                pltpu.VMEM((2 * count, 8, 128), jnp.float32),
-                pltpu.VMEM((degrees // 128, 8 * (2 * count + PAD), 128), jnp.float32),
-                pltpu.VMEM((width // 128, 8 * (2 * count + PAD), 128), jnp.float32),
-            ],
+            in_specs=in_specs,
+            out_specs=out_specs,
+            scratch_shapes=scratch,
         ),
         compiler_params=pltpu.CompilerParams(vmem_limit_bytes=VMEM_LIMIT),
         cost_estimate=pl.CostEstimate(
@@ -373,7 +408,8 @@
             transcendentals=pairs * padded * degrees,
             bytes_accessed=4 * padded * degrees * width + 16 * count * padded * degrees,
         ),
-    )(me, *parts, targets, band, *[array for pair in tables for array in pair])
+    )(*scalars, *parts, targets.transpose(0, 2, 1, 3), band, *extra)
+    return outs[0] if build is None else (outs[0], (outs[1], outs[2]))
 
 
 def longitude_kernel(count, *refs):
@@ -544,19 +580,25 @@
     for cut in early:
         arrived.append(exchange(cut))
     for number, (chunk, first, last) in enumerate(items[2:], 2):
-        source, *arrived[-1] = lax.optimization_barrier((members, *arrived[-1]))
-        arrived.append(exchange(pieces(source, chunk, [(first, last)])[0]))
+        cut = pieces(members, chunk, [(first, last)])[0]
+        cut, arrived[-1] = lax.optimization_barrier((cut, arrived[-1]))
+        arrived.append(exchange(cut))
 
     tables = {}
     received = []
     for number, (chunk, first, last) in enumerate(items):
-        if number < 2:
-            tables[number] = legendre_tables(mine[first:last], degrees, lat_rows, valid)
-        used = [tables[number]] if number < 2 else [tables[0], tables[1]]
         count = min(last, slots) - first
-        payload = lat_payload(
-            index, count, arrived[number], target, chunk, first // 8, used, spaces
-        )
+        place = (target, chunk, first // 8)
+        if number == 0:
+            tables[0] = legendre_tables(mine[first:last], degrees, lat_rows, valid)
+        if number == 1:
+            build = table_inputs(mine[first:last], degrees, lat_rows, valid)
+            payload, tables[1] = lat_payload(
+                index, count, arrived[number], *place, None, spaces, build
+            )
+        else:
+            used = [tables[0]] if number == 0 else [tables[0], tables[1]]
+            payload = lat_payload(index, count, arrived[number], *place, used, spaces)
         if number == 0:
             payload, mine = lax.optimization_barrier((payload, mine))
         blocks = payload.reshape(groups * spaces, last - first, payload.shape[3])

time: 409 us -> 397 us (0.971)
  blocking collectives: 36.5 us -> 0 us
  waiting for transfers between devices: 134 us -> 153 us
  starting transfers between devices: 43.1 us -> 57.2 us
  Pallas kernels: 171 us -> 165 us
    all_to_all x1 -> x0, blocking collectives: 36.5 us -> none  [shards(): moved = lax.all_to_all(blocks, ('member', 'space'), 0, 0, tiled=True)]
    ppermute x15, waiting for transfers between devices: 115 us -> 133 us  [exchange(): lax.ppermute(cut[step], 'member', [(i, (i + step) % groups) for i in rang...]
    pallas_call x2 -> x1, Pallas kernels: 27.6 us -> 13 us  [legendre_tables(): pl.pallas_call(table_kernel, name='legendre_table', out_shape=(shape, sha...]
    all_to_all x4 -> x5, starting transfers between devices: 28.4 us -> 39.8 us  [shards(): moved = lax.all_to_all(blocks, ('member', 'space'), 0, 0, tiled=True)]
    pallas_call x5, Pallas kernels: 90.8 us -> 100 us  [lat_payload(): pl.pallas_call(kernel, name='loss_gradient', out_shape=out_shape, grid_sp...]
    all_to_all x4 -> x5, waiting for transfers between devices: 19.4 us -> 19.4 us  [shards(): moved = lax.all_to_all(blocks, ('member', 'space'), 0, 0, tiled=True)]
  transfers between devices with their start and end apart: 19 -> 20, of which waited for: 10 -> 13; matrix products, arithmetic and copies ran while one was open for 5% -> 5% of each run, Pallas kernels for 32% -> 35%
where the time goes in v3:
time: 397 us; the launch traced here: 396 us
  Pallas kernels  165 us (42%)
  waiting for transfers between devices  153 us (39%)
  starting transfers between devices  57.2 us (14%)
  other arithmetic  17.7 us (4%)
    ppermute x15, waiting for transfers between devices, exchange(): lax.ppermute(cut[step], 'member', [(i, (i + step) % groups) for i in rang...  133 us
    pallas_call x5, Pallas kernels, lat_payload(): pl.pallas_call(kernel, name='loss_gradient', out_shape=out_shape, grid_sp...  100 us
    all_to_all x5, starting transfers between devices, shards(): moved = lax.all_to_all(blocks, ('member', 'space'), 0, 0, tiled=True)  39.8 us
    pallas_call x3, Pallas kernels, to_longitudes(): pl.pallas_call(functools.partial(longitude_kernel, len(received)), name='...  21.8 us
    all_to_all x5, waiting for transfers between devices, shards(): moved = lax.all_to_all(blocks, ('member', 'space'), 0, 0, tiled=True)  19.4 us
    pallas_call x4, Pallas kernels, cut_pieces(): pl.pallas_call(functools.partial(cut_kernel, bounds), name='cut_pieces',...  19.3 us
    ppermute x15, starting transfers between devices, exchange(): lax.ppermute(cut[step], 'member', [(i, (i + step) % groups) for i in rang...  17.4 us
    pallas_call x1, Pallas kernels, legendre_tables(): pl.pallas_call(table_kernel, name='legendre_table', out_shape=(shape, sha...  13 us
  transfers between devices with their start and end apart: 20, of which 13 were waited for; matrix products, arithmetic and copies ran while one was open for 5% of the time, Pallas kernels for 35%

profile of v3, /device:TPU:0, one launch (start us, length us, event | category | flops | bytes accessed | tf_op | source)
XLA Modules:
  0.0 395.8 jit_solution(7582549209205152667)
XLA Ops:
  0.6 5.0 %cut_pieces.7 = (f32[4,2,24,384]{3,2,1,0:T(8,128)}, f32[4,2,24,384]{3,2,1,0:T(8,128)}, f32[4,2,24,384]{3,2,1,0:T(8,128)}, f32[4,2,24,384]{3,2,1,0:T(8,128)}, f32...) custom-call(s32[4]{0:T(128)} %get-tuple-element.127._, ...), custom_call_target="tpu_custom_call" | custom-call | bytes 4521984 | tf_op jit(solution)/shard_map/cut_pieces/pallas_call | solution.py:181
  6.1 2.6 collective-permute-start.13
  8.7 1.4 collective-permute-start.14
  10.4 0.7 floor_minimum_fusion.1
  13.0 13.0 %legendre_table.1 = (bf16[24,384,384]{2,1,0:T(8,128)(2,1)}, bf16[24,384,384]{2,1,0:T(8,128)(2,1)}) custom-call(f32[384]{0:T(512)} %copy-done, f32[384]{0:T(512)} %maximum_divide_fusion.inv_ref, f32[24,128]{1,0:T(8,128)} %broadcast_in_dim.73.order_ref, f32[24,384]{1,0:T(8,128)} %get-tuple-element.118.value_ref, f32[24,384]{1,0:T(8,128)} %get-tuple-element.117.scale_ref, ...), custom_call_target="tpu_custom_call" | custom-call | flops 35389440 | bytes 14155776 | tf_op jit(solution)/shard_map/legendre_table/pallas_call | solution.py:142
  26.7 11.7 %loss_gradient.5 = f32[4,8,24,384]{3,2,1,0:T(8,128)} custom-call(s32[1]{0:T(128)} %bitcast.me_ref, f32[4,2,24,384]{3,2,1,0:T(8,128)} %get-tuple-element.90.refs_0_, f32[4,2,24,384]{3,2,1,0:T(8,128)} %collective-permute-done.12.refs_1_, f32[4,2,24,384]{3,2,1,0:T(8,128)} %collective-permute-done.13.refs_2_, f32[4,2,24,384]{3,2,1,0:T(8,128)} %collective-permute-done.14.refs_3_, ...), custom_call_target="tpu_custom_call" | custom-call | flops 679477248 | bytes 16515072 | tf_op jit(solution)/shard_map/loss_gradient/pallas_call | solution.py:394
  38.3 5.0 %all-to-all-start.1 = ((f32[32,24,384]{2,1,0:T(8,128)}), f32[32,24,384]{2,1,0:T(8,128)}, u32[]{:S(2)}, u32[]{:S(2)}) async-start(f32[32,24,384]{2,1,0:T(8,128)} %bitcast.52), calls=%async_computation.1 | async-start | bytes 2359296 | tf_op jit(solution)/shard_map/all_to_all | solution.py:605
  43.6 1.6 collective-permute-start.1
  45.2 1.4 collective-permute-start.2
  46.6 4.8 %cut_pieces.6 = (f32[4,2,48,384]{3,2,1,0:T(8,128)}, f32[4,2,48,384]{3,2,1,0:T(8,128)}, f32[4,2,48,384]{3,2,1,0:T(8,128)}, f32[4,2,48,384]{3,2,1,0:T(8,128)}) custom-call(s32[4]{0:T(128)} %get-tuple-element.128._, f32[4,16,46,2,384]{4,3,2,1,0:T(2,128)} %bitcast.32, f32[4,16,46,2,384]{4,3,2,1,0:T(2,128)} %bitcast.33, f32[4,16,46,2,384]{4,3,2,1,0:T(2,128)} %bitcast.34, ...), custom_call_target="tpu_custom_call" | custom-call | bytes 4521984 | tf_op jit(solution)/shard_map/cut_pieces/pallas_call | solution.py:181
  51.4 9.9 %collective-permute-done.refs_1_ = f32[4,2,24,384]{3,2,1,0:T(8,128)} collective-permute-done((f32[4,2,24,384]{3,2,1,0:T(8,128)}, f32[4,2,24,384]{3,2,1,0:T(8,128)}, u32[]{:S(2)}, u32[]{:S(2)}) %collective-permute-start) | collective-permute-done | bytes 294944 | tf_op jit(solution)/shard_map/ppermute | solution.py:569
  61.3 1.7 collective-permute-done.1.refs_2_
  63.0 4.9 %collective-permute-done.2.refs_3_ = f32[4,2,24,384]{3,2,1,0:T(8,128)} collective-permute-done((f32[4,2,24,384]{3,2,1,0:T(8,128)}, f32[4,2,24,384]{3,2,1,0:T(8,128)}, u32[]{:S(2)}, u32[]{:S(2)}) %collective-permute-start.2) | collective-permute-done | bytes 294944 | tf_op jit(solution)/shard_map/ppermute | solution.py:569
  69.4 21.5 %loss_gradient.6 = (f32[4,8,24,384]{3,2,1,0:T(8,128)}, bf16[24,384,384]{2,1,0:T(8,128)(2,1)}, bf16[24,384,384]{2,1,0:T(8,128)(2,1)}) custom-call(s32[1]{0:T(128)} %bitcast.me_ref, f32[384]{0:T(512)} %copy-done, f32[384]{0:T(512)} %maximum_divide_fusion.inv_ref, f32[4,2,24,384]{3,2,1,0:T(8,128)} %get-tuple-element.86.refs_0_, ...), custom_call_target="tpu_custom_call" | custom-call | flops 679477248 | bytes 16515072 | tf_op jit(solution)/shard_map/loss_gradient/pallas_call | solution.py:394
  90.9 7.8 %all-to-all-start.2 = ((f32[32,24,384]{2,1,0:T(8,128)}), f32[32,24,384]{2,1,0:T(8,128)}, u32[]{:S(2)}, u32[]{:S(2)}) async-start(f32[32,24,384]{2,1,0:T(8,128)} %bitcast.56), calls=%async_computation.2 | async-start | bytes 2359296 | tf_op jit(solution)/shard_map/all_to_all | solution.py:605
  99.0 1.6 collective-permute-start.4
  100.7 1.4 collective-permute-start.5
  102.6 4.7 %cut_pieces.5 = (f32[4,2,48,384]{3,2,1,0:T(8,128)}, f32[4,2,48,384]{3,2,1,0:T(8,128)}, f32[4,2,48,384]{3,2,1,0:T(8,128)}, f32[4,2,48,384]{3,2,1,0:T(8,128)}) custom-call(s32[4]{0:T(128)} %get-tuple-element.129._, f32[4,16,46,2,384]{4,3,2,1,0:T(2,128)} %bitcast.36, f32[4,16,46,2,384]{4,3,2,1,0:T(2,128)} %bitcast.37, f32[4,16,46,2,384]{4,3,2,1,0:T(2,128)} %bitcast.38, ...), custom_call_target="tpu_custom_call" | custom-call | bytes 4521984 | tf_op jit(solution)/shard_map/cut_pieces/pallas_call | solution.py:181
  107.4 17.4 %collective-permute-done.3.refs_1_ = f32[4,2,48,384]{3,2,1,0:T(8,128)} collective-permute-done((f32[4,2,48,384]{3,2,1,0:T(8,128)}, f32[4,2,48,384]{3,2,1,0:T(8,128)}, u32[]{:S(2)}, u32[]{:S(2)}) %collective-permute-start.3) | collective-permute-done | bytes 589856 | tf_op jit(solution)/shard_map/ppermute | solution.py:569
  124.7 1.5 collective-permute-done.4.refs_2_
  126.3 11.2 %collective-permute-done.5.refs_3_ = f32[4,2,48,384]{3,2,1,0:T(8,128)} collective-permute-done((f32[4,2,48,384]{3,2,1,0:T(8,128)}, f32[4,2,48,384]{3,2,1,0:T(8,128)}, u32[]{:S(2)}, u32[]{:S(2)}) %collective-permute-start.5) | collective-permute-done | bytes 589856 | tf_op jit(solution)/shard_map/ppermute | solution.py:569
  137.4 22.3 %loss_gradient.8 = f32[4,8,48,384]{3,2,1,0:T(8,128)} custom-call(s32[1]{0:T(128)} %bitcast.me_ref, f32[4,2,48,384]{3,2,1,0:T(8,128)} %get-tuple-element.99.refs_0_, f32[4,2,48,384]{3,2,1,0:T(8,128)} %collective-permute-done.3.refs_1_, f32[4,2,48,384]{3,2,1,0:T(8,128)} %collective-permute-done.4.refs_2_, f32[4,2,48,384]{3,2,1,0:T(8,128)} %collective-permute-done.5.refs_3_, ...), custom_call_target="tpu_custom_call" | custom-call | flops 1358954496 | bytes 33030144 | tf_op jit(solution)/shard_map/loss_gradient/pallas_call | solution.py:394
  159.8 6.3 %all-to-all-start.3 = ((f32[32,48,384]{2,1,0:T(8,128)}), f32[32,48,384]{2,1,0:T(8,128)}, u32[]{:S(2)}, u32[]{:S(2)}) async-start(f32[32,48,384]{2,1,0:T(8,128)} %bitcast.45), calls=%async_computation.3 | async-start | bytes 4718592 | tf_op jit(solution)/shard_map/all_to_all | solution.py:605
  166.3 1.6 collective-permute-start.7
  167.9 1.4 collective-permute-start.8
  169.3 4.8 %cut_pieces.4 = (f32[4,2,48,384]{3,2,1,0:T(8,128)}, f32[4,2,48,384]{3,2,1,0:T(8,128)}, f32[4,2,48,384]{3,2,1,0:T(8,128)}, f32[4,2,48,384]{3,2,1,0:T(8,128)}) custom-call(s32[4]{0:T(128)} %get-tuple-element.130._, f32[4,16,46,2,384]{4,3,2,1,0:T(2,128)} %bitcast.40, f32[4,16,46,2,384]{4,3,2,1,0:T(2,128)} %bitcast.41, f32[4,16,46,2,384]{4,3,2,1,0:T(2,128)} %bitcast.42, ...), custom_call_target="tpu_custom_call" | custom-call | bytes 4521984 | tf_op jit(solution)/shard_map/cut_pieces/pallas_call | solution.py:181
  174.1 26.7 %collective-permute-done.6.refs_1_ = f32[4,2,48,384]{3,2,1,0:T(8,128)} collective-permute-done((f32[4,2,48,384]{3,2,1,0:T(8,128)}, f32[4,2,48,384]{3,2,1,0:T(8,128)}, u32[]{:S(2)}, u32[]{:S(2)}) %collective-permute-start.6) | collective-permute-done | bytes 589856 | tf_op jit(solution)/shard_map/ppermute | solution.py:569
  200.7 1.9 collective-permute-done.7.refs_2_
  202.6 12.4 %collective-permute-done.8.refs_3_ = f32[4,2,48,384]{3,2,1,0:T(8,128)} collective-permute-done((f32[4,2,48,384]{3,2,1,0:T(8,128)}, f32[4,2,48,384]{3,2,1,0:T(8,128)}, u32[]{:S(2)}, u32[]{:S(2)}) %collective-permute-start.8) | collective-permute-done | bytes 589856 | tf_op jit(solution)/shard_map/ppermute | solution.py:569
  215.0 22.3 %loss_gradient.9 = f32[4,8,48,384]{3,2,1,0:T(8,128)} custom-call(s32[1]{0:T(128)} %bitcast.me_ref, f32[4,2,48,384]{3,2,1,0:T(8,128)} %get-tuple-element.103.refs_0_, f32[4,2,48,384]{3,2,1,0:T(8,128)} %collective-permute-done.6.refs_1_, f32[4,2,48,384]{3,2,1,0:T(8,128)} %collective-permute-done.7.refs_2_, f32[4,2,48,384]{3,2,1,0:T(8,128)} %collective-permute-done.8.refs_3_, ...), custom_call_target="tpu_custom_call" | custom-call | flops 1358954496 | bytes 33030144 | tf_op jit(solution)/shard_map/loss_gradient/pallas_call | solution.py:394
  237.3 10.2 %all-to-all-start.4 = ((f32[32,48,384]{2,1,0:T(8,128)}), f32[32,48,384]{2,1,0:T(8,128)}, u32[]{:S(2)}, u32[]{:S(2)}) async-start(f32[32,48,384]{2,1,0:T(8,128)} %bitcast.46), calls=%async_computation.4 | async-start | bytes 4718592 | tf_op jit(solution)/shard_map/all_to_all | solution.py:605
  247.8 1.6 collective-permute-start.10
  249.4 1.4 collective-permute-start.11
  250.7 31.4 %collective-permute-done.9.refs_1_ = f32[4,2,48,384]{3,2,1,0:T(8,128)} collective-permute-done((f32[4,2,48,384]{3,2,1,0:T(8,128)S(1)}, f32[4,2,48,384]{3,2,1,0:T(8,128)}, u32[]{:S(2)}, u32[]{:S(2)}) %collective-permute-start.9) | collective-permute-done | bytes 589856 | tf_op jit(solution)/shard_map/ppermute | solution.py:569
  282.1 1.9 collective-permute-done.10.refs_2_
  284.1 12.2 %collective-permute-done.11.refs_3_ = f32[4,2,48,384]{3,2,1,0:T(8,128)} collective-permute-done((f32[4,2,48,384]{3,2,1,0:T(8,128)S(1)}, f32[4,2,48,384]{3,2,1,0:T(8,128)}, u32[]{:S(2)}, u32[]{:S(2)}) %collective-permute-start.11) | collective-permute-done | bytes 589856 | tf_op jit(solution)/shard_map/ppermute | solution.py:569
  296.3 22.3 %loss_gradient.7 = f32[4,8,48,384]{3,2,1,0:T(8,128)} custom-call(s32[1]{0:T(128)} %bitcast.me_ref, f32[4,2,48,384]{3,2,1,0:T(8,128)} %get-tuple-element.80.refs_0_, f32[4,2,48,384]{3,2,1,0:T(8,128)} %collective-permute-done.9.refs_1_, f32[4,2,48,384]{3,2,1,0:T(8,128)} %collective-permute-done.10.refs_2_, f32[4,2,48,384]{3,2,1,0:T(8,128)} %collective-permute-done.11.refs_3_, ...), custom_call_target="tpu_custom_call" | custom-call | flops 1358954496 | bytes 33030144 | tf_op jit(solution)/shard_map/loss_gradient/pallas_call | solution.py:394
  318.6 10.5 %all-to-all-start = ((f32[32,48,384]{2,1,0:T(8,128)}), f32[32,48,384]{2,1,0:T(8,128)}, u32[]{:S(2)}, u32[]{:S(2)}) async-start(f32[32,48,384]{2,1,0:T(8,128)} %bitcast.44), calls=%async_computation | async-start | bytes 4718592 | tf_op jit(solution)/shard_map/all_to_all | solution.py:605
  329.4 5.2 %select_multiply_fusion.1 = (f32[384,720]{1,0:T(8,128)S(1)}, f32[384,720]{1,0:T(8,128)S(1)}) fusion(s32[384]{0:T(512)S(1)} %reshape.277, pred[384]{0:T(512)(128)(4,1)S(1)} %broadcast_compare_fusion), kind=kLoop, calls=%fused_computation.16 | loop fusion | flops 3870720 | bytes 2213760 | tf_op jit(solution)/shard_map/mul | solution.py:536
  334.7 1.8 fusion
  336.4 2.6 select_multiply_fusion.5
  339.1 2.6 select_multiply_fusion.3
  341.7 1.6 fusion.1
  343.4 7.9 %longitudes.3 = f32[4,192,720]{2,1,0:T(8,128)} custom-call(f32[4,192,384]{2,1,0:T(8,128)} %bitcast.9.refs_0_, f32[4,192,384]{2,1,0:T(8,128)} %bitcast.11.refs_1_, bf16[384,720]{1,0:T(8,128)(2,1)} %get-tuple-element.112.refs_2_, bf16[384,720]{1,0:T(8,128)(2,1)} %get-tuple-element.111.refs_3_, bf16[384,720]{1,0:T(8,128)(2,1)} %get-tuple-element.133.refs_4_, ...), custom_call_target="tpu_custom_call" | custom-call | flops 2548039680 | bytes 4571136 | tf_op jit(solution)/shard_map/longitudes/pallas_call | solution.py:434
  351.3 6.9 %longitudes.4 = f32[4,192,720]{2,1,0:T(8,128)} custom-call(f32[4,384,384]{2,1,0:T(8,128)} %bitcast.14.refs_0_, bf16[768,720]{1,0:T(8,128)(2,1)} %get-tuple-element.108.refs_1_.high_ref, bf16[768,720]{1,0:T(8,128)(2,1)} %get-tuple-element.107.refs_2_.low_ref), custom_call_target="tpu_custom_call" | custom-call | flops 2548039680 | bytes 4571136 | tf_op jit(solution)/shard_map/longitudes/pallas_call | solution.py:434
  358.3 6.9 %longitudes.5 = f32[4,192,720]{2,1,0:T(8,128)} custom-call(f32[4,384,384]{2,1,0:T(8,128)} %bitcast.17.refs_0_, bf16[768,720]{1,0:T(8,128)(2,1)} %get-tuple-element.108.refs_1_.high_ref, bf16[768,720]{1,0:T(8,128)(2,1)} %get-tuple-element.107.refs_2_.low_ref), custom_call_target="tpu_custom_call" | custom-call | flops 2548039680 | bytes 4571136 | tf_op jit(solution)/shard_map/longitudes/pallas_call | solution.py:434
  365.2 19.4 %all-to-all-done = f32[32,48,384]{2,1,0:T(8,128)} async-done(((f32[32,48,384]{2,1,0:T(8,128)}), f32[32,48,384]{2,1,0:T(8,128)}, u32[]{:S(2)}, u32[]{:S(2)}) %all-to-all-start) | async-done | bytes 2359328 | tf_op jit(solution)/shard_map/all_to_all | solution.py:605
  384.6 11.2 %merge_channels.1 = f32[4,736,720]{2,1,0:T(8,128)} custom-call(f32[4,384,384]{2,1,0:T(8,128)} %bitcast.7.got_ref, bf16[768,720]{1,0:T(8,128)(2,1)} %get-tuple-element.108.refs_1_.high_ref, bf16[768,720]{1,0:T(8,128)(2,1)} %get-tuple-element.107.refs_2_.low_ref, f32[4,4,48,720]{3,2,1,0:T(8,128)} %bitcast.53, f32[4,4,48,720]{3,2,1,0:T(8,128)} %bitcast.54, ...), custom_call_target="tpu_custom_call" | custom-call | flops 2548039680 | bytes 16957440 | tf_op jit(solution)/shard_map/merge_channels/pallas_call | solution.py:504
  (50 shorter events, 7.5 us)
Async XLA Ops:
  0.6 9.5 %copy-start.1 = (s32[368]{0:T(512)S(1)}, s32[368]{0:T(512)}, u32[]{:S(2)}) copy-start(s32[368]{0:T(512)} %param.5) | copy-start | bytes 4420
  5.6 20.5 %collective-permute-start.12 = (f32[4,2,24,384]{3,2,1,0:T(8,128)}, f32[4,2,24,384]{3,2,1,0:T(8,128)}, u32[]{:S(2)}, u32[]{:S(2)}) collective-permute-start(f32[4,2,24,384]{3,2,1,0:T(8,128)} %get-tuple-element.91), channel_id=1, source_target_pairs={{0,8},{8,16},{16,24},{24,0},{1,9},{9,17},{17,25},{25,1},{2,10},{10... | collective-permute-start | bytes 884744 | tf_op jit(solution)/shard_map/ppermute | solution.py:569
  6.1 19.9 %collective-permute-start.13 = (f32[4,2,24,384]{3,2,1,0:T(8,128)}, f32[4,2,24,384]{3,2,1,0:T(8,128)}, u32[]{:S(2)}, u32[]{:S(2)}) collective-permute-start(f32[4,2,24,384]{3,2,1,0:T(8,128)} %get-tuple-element.92), channel_id=1, source_target_pairs={{0,16},{8,24},{16,0},{24,8},{1,17},{9,25},{17,1},{25,9},{2,18},{10... | collective-permute-start | bytes 884744 | tf_op jit(solution)/shard_map/ppermute | solution.py:569
  8.7 17.4 %collective-permute-start.14 = (f32[4,2,24,384]{3,2,1,0:T(8,128)}, f32[4,2,24,384]{3,2,1,0:T(8,128)}, u32[]{:S(2)}, u32[]{:S(2)}) collective-permute-start(f32[4,2,24,384]{3,2,1,0:T(8,128)} %get-tuple-element.93), channel_id=1, source_target_pairs={{0,24},{8,0},{16,8},{24,16},{1,25},{9,1},{17,9},{25,17},{2,26},{10... | collective-permute-start | bytes 884744 | tf_op jit(solution)/shard_map/ppermute | solution.py:569
  10.1 3.0 copy-start
  38.3 52.6 %all-to-all-start.1 = ((f32[32,24,384]{2,1,0:T(8,128)}), f32[32,24,384]{2,1,0:T(8,128)}, u32[]{:S(2)}, u32[]{:S(2)}) async-start(f32[32,24,384]{2,1,0:T(8,128)} %bitcast.52), calls=%async_computation.1 | async-start | bytes 2359296 | tf_op jit(solution)/shard_map/all_to_all | solution.py:605
  43.4 17.9 %collective-permute-start = (f32[4,2,24,384]{3,2,1,0:T(8,128)}, f32[4,2,24,384]{3,2,1,0:T(8,128)}, u32[]{:S(2)}, u32[]{:S(2)}) collective-permute-start(f32[4,2,24,384]{3,2,1,0:T(8,128)} %get-tuple-element.69), channel_id=1, source_target_pairs={{0,8},{8,16},{16,24},{24,0},{1,9},{9,17},{17,25},{25,1},{2,10},{10... | collective-permute-start | bytes 884744 | tf_op jit(solution)/shard_map/ppermute | solution.py:569
  43.6 19.4 %collective-permute-start.1 = (f32[4,2,24,384]{3,2,1,0:T(8,128)}, f32[4,2,24,384]{3,2,1,0:T(8,128)}, u32[]{:S(2)}, u32[]{:S(2)}) collective-permute-start(f32[4,2,24,384]{3,2,1,0:T(8,128)} %get-tuple-element.70), channel_id=1, source_target_pairs={{0,16},{8,24},{16,0},{24,8},{1,17},{9,25},{17,1},{25,9},{2,18},{10... | collective-permute-start | bytes 884744 | tf_op jit(solution)/shard_map/ppermute | solution.py:569
  45.2 22.6 %collective-permute-start.2 = (f32[4,2,24,384]{3,2,1,0:T(8,128)}, f32[4,2,24,384]{3,2,1,0:T(8,128)}, u32[]{:S(2)}, u32[]{:S(2)}) collective-permute-start(f32[4,2,24,384]{3,2,1,0:T(8,128)} %get-tuple-element.71), channel_id=1, source_target_pairs={{0,24},{8,0},{16,8},{24,16},{1,25},{9,1},{17,9},{25,17},{2,26},{10... | collective-permute-start | bytes 884744 | tf_op jit(solution)/shard_map/ppermute | solution.py:569
  90.9 68.8 %all-to-all-start.2 = ((f32[32,24,384]{2,1,0:T(8,128)}), f32[32,24,384]{2,1,0:T(8,128)}, u32[]{:S(2)}, u32[]{:S(2)}) async-start(f32[32,24,384]{2,1,0:T(8,128)} %bitcast.56), calls=%async_computation.2 | async-start | bytes 2359296 | tf_op jit(solution)/shard_map/all_to_all | solution.py:605
  98.8 25.9 %collective-permute-start.3 = (f32[4,2,48,384]{3,2,1,0:T(8,128)}, f32[4,2,48,384]{3,2,1,0:T(8,128)}, u32[]{:S(2)}, u32[]{:S(2)}) collective-permute-start(f32[4,2,48,384]{3,2,1,0:T(8,128)} %get-tuple-element.73), channel_id=1, source_target_pairs={{0,8},{8,16},{16,24},{24,0},{1,9},{9,17},{17,25},{25,1},{2,10},{10... | collective-permute-start | bytes 1769480 | tf_op jit(solution)/shard_map/ppermute | solution.py:569
  99.0 27.2 %collective-permute-start.4 = (f32[4,2,48,384]{3,2,1,0:T(8,128)}, f32[4,2,48,384]{3,2,1,0:T(8,128)}, u32[]{:S(2)}, u32[]{:S(2)}) collective-permute-start(f32[4,2,48,384]{3,2,1,0:T(8,128)} %get-tuple-element.74), channel_id=1, source_target_pairs={{0,16},{8,24},{16,0},{24,8},{1,17},{9,25},{17,1},{25,9},{2,18},{10... | collective-permute-start | bytes 1769480 | tf_op jit(solution)/shard_map/ppermute | solution.py:569
  100.7 36.8 %collective-permute-start.5 = (f32[4,2,48,384]{3,2,1,0:T(8,128)}, f32[4,2,48,384]{3,2,1,0:T(8,128)}, u32[]{:S(2)}, u32[]{:S(2)}) collective-permute-start(f32[4,2,48,384]{3,2,1,0:T(8,128)} %get-tuple-element.75), channel_id=1, source_target_pairs={{0,24},{8,0},{16,8},{24,16},{1,25},{9,1},{17,9},{25,17},{2,26},{10... | collective-permute-start | bytes 1769480 | tf_op jit(solution)/shard_map/ppermute | solution.py:569
  159.8 77.5 %all-to-all-start.3 = ((f32[32,48,384]{2,1,0:T(8,128)}), f32[32,48,384]{2,1,0:T(8,128)}, u32[]{:S(2)}, u32[]{:S(2)}) async-start(f32[32,48,384]{2,1,0:T(8,128)} %bitcast.45), calls=%async_computation.3 | async-start | bytes 4718592 | tf_op jit(solution)/shard_map/all_to_all | solution.py:605
  166.1 34.6 %collective-permute-start.6 = (f32[4,2,48,384]{3,2,1,0:T(8,128)}, f32[4,2,48,384]{3,2,1,0:T(8,128)}, u32[]{:S(2)}, u32[]{:S(2)}) collective-permute-start(f32[4,2,48,384]{3,2,1,0:T(8,128)} %get-tuple-element.77), channel_id=1, source_target_pairs={{0,8},{8,16},{16,24},{24,0},{1,9},{9,17},{17,25},{25,1},{2,10},{10... | collective-permute-start | bytes 1769480 | tf_op jit(solution)/shard_map/ppermute | solution.py:569
  166.3 36.3 %collective-permute-start.7 = (f32[4,2,48,384]{3,2,1,0:T(8,128)}, f32[4,2,48,384]{3,2,1,0:T(8,128)}, u32[]{:S(2)}, u32[]{:S(2)}) collective-permute-start(f32[4,2,48,384]{3,2,1,0:T(8,128)} %get-tuple-element.78), channel_id=1, source_target_pairs={{0,16},{8,24},{16,0},{24,8},{1,17},{9,25},{17,1},{25,9},{2,18},{10... | collective-permute-start | bytes 1769480 | tf_op jit(solution)/shard_map/ppermute | solution.py:569
  167.9 47.1 %collective-permute-start.8 = (f32[4,2,48,384]{3,2,1,0:T(8,128)}, f32[4,2,48,384]{3,2,1,0:T(8,128)}, u32[]{:S(2)}, u32[]{:S(2)}) collective-permute-start(f32[4,2,48,384]{3,2,1,0:T(8,128)} %get-tuple-element.79), channel_id=1, source_target_pairs={{0,24},{8,0},{16,8},{24,16},{1,25},{9,1},{17,9},{25,17},{2,26},{10... | collective-permute-start | bytes 1769480 | tf_op jit(solution)/shard_map/ppermute | solution.py:569
  237.3 10.2 %copy-start.4 = (f32[4,2,48,384]{3,2,1,0:T(8,128)S(1)}, f32[4,2,48,384]{3,2,1,0:T(8,128)}, u32[]{:S(2)}) copy-start(f32[4,2,48,384]{3,2,1,0:T(8,128)} %get-tuple-element.81) | copy-start | bytes 1769476
  237.3 10.5 %copy-start.3 = (f32[4,2,48,384]{3,2,1,0:T(8,128)S(1)}, f32[4,2,48,384]{3,2,1,0:T(8,128)}, u32[]{:S(2)}) copy-start(f32[4,2,48,384]{3,2,1,0:T(8,128)} %get-tuple-element.82) | copy-start | bytes 1769476
  237.3 12.1 %copy-start.2 = (f32[4,2,48,384]{3,2,1,0:T(8,128)S(1)}, f32[4,2,48,384]{3,2,1,0:T(8,128)}, u32[]{:S(2)}) copy-start(f32[4,2,48,384]{3,2,1,0:T(8,128)} %get-tuple-element.83) | copy-start | bytes 1769476
  237.3 81.3 %all-to-all-start.4 = ((f32[32,48,384]{2,1,0:T(8,128)}), f32[32,48,384]{2,1,0:T(8,128)}, u32[]{:S(2)}, u32[]{:S(2)}) async-start(f32[32,48,384]{2,1,0:T(8,128)} %bitcast.46), calls=%async_computation.4 | async-start | bytes 4718592 | tf_op jit(solution)/shard_map/all_to_all | solution.py:605
  247.5 34.6 %collective-permute-start.9 = (f32[4,2,48,384]{3,2,1,0:T(8,128)S(1)}, f32[4,2,48,384]{3,2,1,0:T(8,128)}, u32[]{:S(2)}, u32[]{:S(2)}) collective-permute-start(f32[4,2,48,384]{3,2,1,0:T(8,128)S(1)} %copy-done.4), channel_id=1, source_target_pairs={{0,8},{8,16},{16,24},{24,0},{1,9},{9,17},{17,25},{25,1},{2,10},{10... | collective-permute-start | bytes 1769480 | tf_op jit(solution)/shard_map/ppermute | solution.py:569
  247.8 36.3 %collective-permute-start.10 = (f32[4,2,48,384]{3,2,1,0:T(8,128)S(1)}, f32[4,2,48,384]{3,2,1,0:T(8,128)}, u32[]{:S(2)}, u32[]{:S(2)}) collective-permute-start(f32[4,2,48,384]{3,2,1,0:T(8,128)S(1)} %copy-done.3), channel_id=1, source_target_pairs={{0,16},{8,24},{16,0},{24,8},{1,17},{9,25},{17,1},{25,9},{2,18},{10... | collective-permute-start | bytes 1769480 | tf_op jit(solution)/shard_map/ppermute | solution.py:569
  249.4 46.9 %collective-permute-start.11 = (f32[4,2,48,384]{3,2,1,0:T(8,128)S(1)}, f32[4,2,48,384]{3,2,1,0:T(8,128)}, u32[]{:S(2)}, u32[]{:S(2)}) collective-permute-start(f32[4,2,48,384]{3,2,1,0:T(8,128)S(1)} %copy-done.2), channel_id=1, source_target_pairs={{0,24},{8,0},{16,8},{24,16},{1,25},{9,1},{17,9},{25,17},{2,26},{10... | collective-permute-start | bytes 1769480 | tf_op jit(solution)/shard_map/ppermute | solution.py:569
  318.6 66.0 %all-to-all-start = ((f32[32,48,384]{2,1,0:T(8,128)}), f32[32,48,384]{2,1,0:T(8,128)}, u32[]{:S(2)}, u32[]{:S(2)}) async-start(f32[32,48,384]{2,1,0:T(8,128)} %bitcast.44), calls=%async_computation | async-start | bytes 4718592 | tf_op jit(solution)/shard_map/all_to_all | solution.py:605

commit v4 on v3

--- a/solution.py
+++ b/solution.py
@@ -162,20 +162,25 @@
 def cut_kernel(bounds, _, *refs):
     count = len(refs) // (1 + len(bounds))
     for index, source in enumerate(refs[:count]):
-        slots = source.shape[0]
+        together, slots = source.shape[:2]
         for cut, (first, last) in enumerate(bounds):
             rows = min(last, slots) - first
-            for part in range(2):
-                refs[count + cut * count + index][part, :rows] = source[first : first + rows, part, :]
+            piece = refs[count + cut * count + index]
+            for member in range(together):
+                for part in range(2):
+                    piece[member, part, :rows] = source[member, first : first + rows, part, :]
 
 
 def cut_pieces(members, channels, bounds):
     local, _, _, slots, degrees = members.shape
     count = channels.shape[0]
+    together = 2 if local % 2 == 0 else 1
     source = members.transpose(0, 1, 3, 2, 4)
 
     def in_spec(piece):
-        return pl.BlockSpec((None, None, slots, 2, degrees), lambda e, picked: (e, picked[piece], 0, 0, 0))
+        return pl.BlockSpec(
+            (together, None, slots, 2, degrees), lambda e, picked: (e, picked[piece], 0, 0, 0)
+        )
 
     shapes = [(2, last - first, degrees) for first, last in bounds for _ in range(count)]
     outs = pl.pallas_call(
@@ -184,9 +189,11 @@
         out_shape=[jax.ShapeDtypeStruct((local, *shape), jnp.float32) for shape in shapes],
         grid_spec=pltpu.PrefetchScalarGridSpec(
             num_scalar_prefetch=1,
-            grid=(local,),
+            grid=(local // together,),
             in_specs=[in_spec(piece) for piece in range(count)],
-            out_specs=[pl.BlockSpec((None, *shape), lambda e, _: (e, 0, 0, 0)) for shape in shapes],
+            out_specs=[
+                pl.BlockSpec((together, *shape), lambda e, _: (e, 0, 0, 0)) for shape in shapes
+            ],
         ),
         compiler_params=pltpu.CompilerParams(vmem_limit_bytes=VMEM_LIMIT),
         cost_estimate=pl.CostEstimate(
@@ -329,7 +336,7 @@
                 out_ref[group, space] = value
         return 0
 
-    lax.fori_loop(0, groups, scatter, 0)
+    lax.fori_loop(0, groups, scatter, 0, unroll=groups if spaces == per else 1)
 
 
 def fused_kernel(slots, groups, me_ref, step_ref, inv_ref, *refs):

time: 397 us -> 385 us (0.970)
  Pallas kernels: 165 us -> 150 us
    pallas_call x5, Pallas kernels: 100 us -> 89.8 us  [lat_payload(): pl.pallas_call(kernel, name='loss_gradient', out_shape=out_shape, grid_sp...]
    pallas_call x4, Pallas kernels: 19.3 us -> 14.3 us  [cut_pieces(): pl.pallas_call(functools.partial(cut_kernel, bounds), name='cut_pieces',...]
  transfers between devices with their start and end apart: 20 -> 20, of which waited for: 13 -> 13; matrix products, arithmetic and copies ran while one was open for 5% -> 5% of each run, Pallas kernels for 35% -> 33%
where the time goes in v4:
time: 385 us; the launch traced here: 384 us
  waiting for transfers between devices  156 us (41%)
  Pallas kernels  150 us (39%)
  starting transfers between devices  57.2 us (15%)
  other arithmetic  17.7 us (5%)
    ppermute x15, waiting for transfers between devices, exchange(): lax.ppermute(cut[step], 'member', [(i, (i + step) % groups) for i in rang...  137 us
    pallas_call x5, Pallas kernels, lat_payload(): pl.pallas_call(kernel, name='loss_gradient', out_shape=out_shape, grid_sp...  89.8 us
    all_to_all x5, starting transfers between devices, shards(): moved = lax.all_to_all(blocks, ('member', 'space'), 0, 0, tiled=True)  39.8 us
    pallas_call x3, Pallas kernels, to_longitudes(): pl.pallas_call(functools.partial(longitude_kernel, len(received)), name='...  21.8 us
    all_to_all x5, waiting for transfers between devices, shards(): moved = lax.all_to_all(blocks, ('member', 'space'), 0, 0, tiled=True)  19.5 us
    ppermute x15, starting transfers between devices, exchange(): lax.ppermute(cut[step], 'member', [(i, (i + step) % groups) for i in rang...  17.4 us
    pallas_call x4, Pallas kernels, cut_pieces(): pl.pallas_call(functools.partial(cut_kernel, bounds), name='cut_pieces',...  14.3 us
    pallas_call x1, Pallas kernels, legendre_tables(): pl.pallas_call(table_kernel, name='legendre_table', out_shape=(shape, sha...  13 us
  transfers between devices with their start and end apart: 20, of which 13 were waited for; matrix products, arithmetic and copies ran while one was open for 5% of the time, Pallas kernels for 33%

profile of v4, /device:TPU:0, one launch (start us, length us, event | category | flops | bytes accessed | tf_op | source)
XLA Modules:
  0.0 384.2 jit_solution(3822935252393315182)
XLA Ops:
  0.6 3.7 cut_pieces.7
  4.8 2.6 collective-permute-start.13
  7.3 1.4 collective-permute-start.14
  9.1 0.7 floor_minimum_fusion.1
  11.7 13.0 %legendre_table.1 = (bf16[24,384,384]{2,1,0:T(8,128)(2,1)}, bf16[24,384,384]{2,1,0:T(8,128)(2,1)}) custom-call(f32[384]{0:T(512)} %copy-done, f32[384]{0:T(512)} %maximum_divide_fusion.inv_ref, f32[24,128]{1,0:T(8,128)} %broadcast_in_dim.73.order_ref, f32[24,384]{1,0:T(8,128)} %get-tuple-element.118.value_ref, f32[24,384]{1,0:T(8,128)} %get-tuple-element.117.scale_ref, ...), custom_call_target="tpu_custom_call" | custom-call | flops 35389440 | bytes 14155776 | tf_op jit(solution)/shard_map/legendre_table/pallas_call | solution.py:142
  25.3 10.3 %loss_gradient.5 = f32[4,8,24,384]{3,2,1,0:T(8,128)} custom-call(s32[1]{0:T(128)} %bitcast.me_ref, f32[4,2,24,384]{3,2,1,0:T(8,128)} %get-tuple-element.90.refs_0_, f32[4,2,24,384]{3,2,1,0:T(8,128)} %collective-permute-done.12.refs_1_, f32[4,2,24,384]{3,2,1,0:T(8,128)} %collective-permute-done.13.refs_2_, f32[4,2,24,384]{3,2,1,0:T(8,128)} %collective-permute-done.14.refs_3_, ...), custom_call_target="tpu_custom_call" | custom-call | flops 679477248 | bytes 16515072 | tf_op jit(solution)/shard_map/loss_gradient/pallas_call | solution.py:401
  35.6 5.0 %all-to-all-start.1 = ((f32[32,24,384]{2,1,0:T(8,128)}), f32[32,24,384]{2,1,0:T(8,128)}, u32[]{:S(2)}, u32[]{:S(2)}) async-start(f32[32,24,384]{2,1,0:T(8,128)} %bitcast.52), calls=%async_computation.1 | async-start | bytes 2359296 | tf_op jit(solution)/shard_map/all_to_all | solution.py:612
  40.9 1.6 collective-permute-start.1
  42.5 1.4 collective-permute-start.2
  43.9 3.6 cut_pieces.6
  47.5 11.1 %collective-permute-done.refs_1_ = f32[4,2,24,384]{3,2,1,0:T(8,128)} collective-permute-done((f32[4,2,24,384]{3,2,1,0:T(8,128)}, f32[4,2,24,384]{3,2,1,0:T(8,128)}, u32[]{:S(2)}, u32[]{:S(2)}) %collective-permute-start) | collective-permute-done | bytes 294944 | tf_op jit(solution)/shard_map/ppermute | solution.py:576
  58.6 1.7 collective-permute-done.1.refs_2_
  60.3 4.9 %collective-permute-done.2.refs_3_ = f32[4,2,24,384]{3,2,1,0:T(8,128)} collective-permute-done((f32[4,2,24,384]{3,2,1,0:T(8,128)}, f32[4,2,24,384]{3,2,1,0:T(8,128)}, u32[]{:S(2)}, u32[]{:S(2)}) %collective-permute-start.2) | collective-permute-done | bytes 294944 | tf_op jit(solution)/shard_map/ppermute | solution.py:576
  66.7 19.0 %loss_gradient.6 = (f32[4,8,24,384]{3,2,1,0:T(8,128)}, bf16[24,384,384]{2,1,0:T(8,128)(2,1)}, bf16[24,384,384]{2,1,0:T(8,128)(2,1)}) custom-call(s32[1]{0:T(128)} %bitcast.me_ref, f32[384]{0:T(512)} %copy-done, f32[384]{0:T(512)} %maximum_divide_fusion.inv_ref, f32[4,2,24,384]{3,2,1,0:T(8,128)} %get-tuple-element.86.refs_0_, ...), custom_call_target="tpu_custom_call" | custom-call | flops 679477248 | bytes 16515072 | tf_op jit(solution)/shard_map/loss_gradient/pallas_call | solution.py:401
  85.7 7.8 %all-to-all-start.2 = ((f32[32,24,384]{2,1,0:T(8,128)}), f32[32,24,384]{2,1,0:T(8,128)}, u32[]{:S(2)}, u32[]{:S(2)}) async-start(f32[32,24,384]{2,1,0:T(8,128)} %bitcast.56), calls=%async_computation.2 | async-start | bytes 2359296 | tf_op jit(solution)/shard_map/all_to_all | solution.py:612
  93.8 1.6 collective-permute-start.4
  95.5 1.4 collective-permute-start.5
  97.4 3.5 cut_pieces.5
  101.0 18.6 %collective-permute-done.3.refs_1_ = f32[4,2,48,384]{3,2,1,0:T(8,128)} collective-permute-done((f32[4,2,48,384]{3,2,1,0:T(8,128)}, f32[4,2,48,384]{3,2,1,0:T(8,128)}, u32[]{:S(2)}, u32[]{:S(2)}) %collective-permute-start.3) | collective-permute-done | bytes 589856 | tf_op jit(solution)/shard_map/ppermute | solution.py:576
  119.6 1.5 collective-permute-done.4.refs_2_
  121.1 11.2 %collective-permute-done.5.refs_3_ = f32[4,2,48,384]{3,2,1,0:T(8,128)} collective-permute-done((f32[4,2,48,384]{3,2,1,0:T(8,128)}, f32[4,2,48,384]{3,2,1,0:T(8,128)}, u32[]{:S(2)}, u32[]{:S(2)}) %collective-permute-start.5) | collective-permute-done | bytes 589856 | tf_op jit(solution)/shard_map/ppermute | solution.py:576
  132.3 20.2 %loss_gradient.8 = f32[4,8,48,384]{3,2,1,0:T(8,128)} custom-call(s32[1]{0:T(128)} %bitcast.me_ref, f32[4,2,48,384]{3,2,1,0:T(8,128)} %get-tuple-element.99.refs_0_, f32[4,2,48,384]{3,2,1,0:T(8,128)} %collective-permute-done.3.refs_1_, f32[4,2,48,384]{3,2,1,0:T(8,128)} %collective-permute-done.4.refs_2_, f32[4,2,48,384]{3,2,1,0:T(8,128)} %collective-permute-done.5.refs_3_, ...), custom_call_target="tpu_custom_call" | custom-call | flops 1358954496 | bytes 33030144 | tf_op jit(solution)/shard_map/loss_gradient/pallas_call | solution.py:401
  152.4 6.3 %all-to-all-start.3 = ((f32[32,48,384]{2,1,0:T(8,128)}), f32[32,48,384]{2,1,0:T(8,128)}, u32[]{:S(2)}, u32[]{:S(2)}) async-start(f32[32,48,384]{2,1,0:T(8,128)} %bitcast.45), calls=%async_computation.3 | async-start | bytes 4718592 | tf_op jit(solution)/shard_map/all_to_all | solution.py:612
  159.0 1.6 collective-permute-start.7
  160.6 1.4 collective-permute-start.8
  162.0 3.5 cut_pieces.4
  165.5 27.9 %collective-permute-done.6.refs_1_ = f32[4,2,48,384]{3,2,1,0:T(8,128)} collective-permute-done((f32[4,2,48,384]{3,2,1,0:T(8,128)}, f32[4,2,48,384]{3,2,1,0:T(8,128)}, u32[]{:S(2)}, u32[]{:S(2)}) %collective-permute-start.6) | collective-permute-done | bytes 589856 | tf_op jit(solution)/shard_map/ppermute | solution.py:576
  193.4 1.9 collective-permute-done.7.refs_2_
  195.3 12.4 %collective-permute-done.8.refs_3_ = f32[4,2,48,384]{3,2,1,0:T(8,128)} collective-permute-done((f32[4,2,48,384]{3,2,1,0:T(8,128)}, f32[4,2,48,384]{3,2,1,0:T(8,128)}, u32[]{:S(2)}, u32[]{:S(2)}) %collective-permute-start.8) | collective-permute-done | bytes 589856 | tf_op jit(solution)/shard_map/ppermute | solution.py:576
  207.7 20.2 %loss_gradient.9 = f32[4,8,48,384]{3,2,1,0:T(8,128)} custom-call(s32[1]{0:T(128)} %bitcast.me_ref, f32[4,2,48,384]{3,2,1,0:T(8,128)} %get-tuple-element.103.refs_0_, f32[4,2,48,384]{3,2,1,0:T(8,128)} %collective-permute-done.6.refs_1_, f32[4,2,48,384]{3,2,1,0:T(8,128)} %collective-permute-done.7.refs_2_, f32[4,2,48,384]{3,2,1,0:T(8,128)} %collective-permute-done.8.refs_3_, ...), custom_call_target="tpu_custom_call" | custom-call | flops 1358954496 | bytes 33030144 | tf_op jit(solution)/shard_map/loss_gradient/pallas_call | solution.py:401
  227.9 10.2 %all-to-all-start.4 = ((f32[32,48,384]{2,1,0:T(8,128)}), f32[32,48,384]{2,1,0:T(8,128)}, u32[]{:S(2)}, u32[]{:S(2)}) async-start(f32[32,48,384]{2,1,0:T(8,128)} %bitcast.46), calls=%async_computation.4 | async-start | bytes 4718592 | tf_op jit(solution)/shard_map/all_to_all | solution.py:612
  238.3 1.6 collective-permute-start.10
  239.9 1.4 collective-permute-start.11
  241.3 31.4 %collective-permute-done.9.refs_1_ = f32[4,2,48,384]{3,2,1,0:T(8,128)} collective-permute-done((f32[4,2,48,384]{3,2,1,0:T(8,128)S(1)}, f32[4,2,48,384]{3,2,1,0:T(8,128)}, u32[]{:S(2)}, u32[]{:S(2)}) %collective-permute-start.9) | collective-permute-done | bytes 589856 | tf_op jit(solution)/shard_map/ppermute | solution.py:576
  272.7 1.9 collective-permute-done.10.refs_2_
  274.6 12.2 %collective-permute-done.11.refs_3_ = f32[4,2,48,384]{3,2,1,0:T(8,128)} collective-permute-done((f32[4,2,48,384]{3,2,1,0:T(8,128)S(1)}, f32[4,2,48,384]{3,2,1,0:T(8,128)}, u32[]{:S(2)}, u32[]{:S(2)}) %collective-permute-start.11) | collective-permute-done | bytes 589856 | tf_op jit(solution)/shard_map/ppermute | solution.py:576
  286.9 20.2 %loss_gradient.7 = f32[4,8,48,384]{3,2,1,0:T(8,128)} custom-call(s32[1]{0:T(128)} %bitcast.me_ref, f32[4,2,48,384]{3,2,1,0:T(8,128)} %get-tuple-element.80.refs_0_, f32[4,2,48,384]{3,2,1,0:T(8,128)} %collective-permute-done.9.refs_1_, f32[4,2,48,384]{3,2,1,0:T(8,128)} %collective-permute-done.10.refs_2_, f32[4,2,48,384]{3,2,1,0:T(8,128)} %collective-permute-done.11.refs_3_, ...), custom_call_target="tpu_custom_call" | custom-call | flops 1358954496 | bytes 33030144 | tf_op jit(solution)/shard_map/loss_gradient/pallas_call | solution.py:401
  307.0 10.5 %all-to-all-start = ((f32[32,48,384]{2,1,0:T(8,128)}), f32[32,48,384]{2,1,0:T(8,128)}, u32[]{:S(2)}, u32[]{:S(2)}) async-start(f32[32,48,384]{2,1,0:T(8,128)} %bitcast.44), calls=%async_computation | async-start | bytes 4718592 | tf_op jit(solution)/shard_map/all_to_all | solution.py:612
  317.9 5.2 %select_multiply_fusion.1 = (f32[384,720]{1,0:T(8,128)S(1)}, f32[384,720]{1,0:T(8,128)S(1)}) fusion(s32[384]{0:T(512)S(1)} %reshape.277, pred[384]{0:T(512)(128)(4,1)S(1)} %broadcast_compare_fusion), kind=kLoop, calls=%fused_computation.16 | loop fusion | flops 3870720 | bytes 2213760 | tf_op jit(solution)/shard_map/mul | solution.py:543
  323.1 1.8 fusion
  324.9 2.6 select_multiply_fusion.5
  327.5 2.6 select_multiply_fusion.3
  330.1 1.6 fusion.1
  331.8 7.9 %longitudes.3 = f32[4,192,720]{2,1,0:T(8,128)} custom-call(f32[4,192,384]{2,1,0:T(8,128)} %bitcast.9.refs_0_, f32[4,192,384]{2,1,0:T(8,128)} %bitcast.11.refs_1_, bf16[384,720]{1,0:T(8,128)(2,1)} %get-tuple-element.112.refs_2_, bf16[384,720]{1,0:T(8,128)(2,1)} %get-tuple-element.111.refs_3_, bf16[384,720]{1,0:T(8,128)(2,1)} %get-tuple-element.133.refs_4_, ...), custom_call_target="tpu_custom_call" | custom-call | flops 2548039680 | bytes 4571136 | tf_op jit(solution)/shard_map/longitudes/pallas_call | solution.py:441
  339.7 6.9 %longitudes.4 = f32[4,192,720]{2,1,0:T(8,128)} custom-call(f32[4,384,384]{2,1,0:T(8,128)} %bitcast.14.refs_0_, bf16[768,720]{1,0:T(8,128)(2,1)} %get-tuple-element.108.refs_1_.high_ref, bf16[768,720]{1,0:T(8,128)(2,1)} %get-tuple-element.107.refs_2_.low_ref), custom_call_target="tpu_custom_call" | custom-call | flops 2548039680 | bytes 4571136 | tf_op jit(solution)/shard_map/longitudes/pallas_call | solution.py:441
  346.7 6.9 %longitudes.5 = f32[4,192,720]{2,1,0:T(8,128)} custom-call(f32[4,384,384]{2,1,0:T(8,128)} %bitcast.17.refs_0_, bf16[768,720]{1,0:T(8,128)(2,1)} %get-tuple-element.108.refs_1_.high_ref, bf16[768,720]{1,0:T(8,128)(2,1)} %get-tuple-element.107.refs_2_.low_ref), custom_call_target="tpu_custom_call" | custom-call | flops 2548039680 | bytes 4571136 | tf_op jit(solution)/shard_map/longitudes/pallas_call | solution.py:441
  353.6 19.4 %all-to-all-done = f32[32,48,384]{2,1,0:T(8,128)} async-done(((f32[32,48,384]{2,1,0:T(8,128)}), f32[32,48,384]{2,1,0:T(8,128)}, u32[]{:S(2)}, u32[]{:S(2)}) %all-to-all-start) | async-done | bytes 2359328 | tf_op jit(solution)/shard_map/all_to_all | solution.py:612
  373.1 11.2 %merge_channels.1 = f32[4,736,720]{2,1,0:T(8,128)} custom-call(f32[4,384,384]{2,1,0:T(8,128)} %bitcast.7.got_ref, bf16[768,720]{1,0:T(8,128)(2,1)} %get-tuple-element.108.refs_1_.high_ref, bf16[768,720]{1,0:T(8,128)(2,1)} %get-tuple-element.107.refs_2_.low_ref, f32[4,4,48,720]{3,2,1,0:T(8,128)} %bitcast.53, f32[4,4,48,720]{3,2,1,0:T(8,128)} %bitcast.54, ...), custom_call_target="tpu_custom_call" | custom-call | flops 2548039680 | bytes 16957440 | tf_op jit(solution)/shard_map/merge_channels/pallas_call | solution.py:511
  (50 shorter events, 7.5 us)
Async XLA Ops:
  0.6 8.2 %copy-start.1 = (s32[368]{0:T(512)S(1)}, s32[368]{0:T(512)}, u32[]{:S(2)}) copy-start(s32[368]{0:T(512)} %param.5) | copy-start | bytes 4420
  4.2 20.5 %collective-permute-start.12 = (f32[4,2,24,384]{3,2,1,0:T(8,128)}, f32[4,2,24,384]{3,2,1,0:T(8,128)}, u32[]{:S(2)}, u32[]{:S(2)}) collective-permute-start(f32[4,2,24,384]{3,2,1,0:T(8,128)} %get-tuple-element.91), channel_id=1, source_target_pairs={{0,8},{8,16},{16,24},{24,0},{1,9},{9,17},{17,25},{25,1},{2,10},{10... | collective-permute-start | bytes 884744 | tf_op jit(solution)/shard_map/ppermute | solution.py:576
  4.8 19.9 %collective-permute-start.13 = (f32[4,2,24,384]{3,2,1,0:T(8,128)}, f32[4,2,24,384]{3,2,1,0:T(8,128)}, u32[]{:S(2)}, u32[]{:S(2)}) collective-permute-start(f32[4,2,24,384]{3,2,1,0:T(8,128)} %get-tuple-element.92), channel_id=1, source_target_pairs={{0,16},{8,24},{16,0},{24,8},{1,17},{9,25},{17,1},{25,9},{2,18},{10... | collective-permute-start | bytes 884744 | tf_op jit(solution)/shard_map/ppermute | solution.py:576
  7.3 17.4 %collective-permute-start.14 = (f32[4,2,24,384]{3,2,1,0:T(8,128)}, f32[4,2,24,384]{3,2,1,0:T(8,128)}, u32[]{:S(2)}, u32[]{:S(2)}) collective-permute-start(f32[4,2,24,384]{3,2,1,0:T(8,128)} %get-tuple-element.93), channel_id=1, source_target_pairs={{0,24},{8,0},{16,8},{24,16},{1,25},{9,1},{17,9},{25,17},{2,26},{10... | collective-permute-start | bytes 884744 | tf_op jit(solution)/shard_map/ppermute | solution.py:576
  8.7 3.0 copy-start
  35.6 50.1 %all-to-all-start.1 = ((f32[32,24,384]{2,1,0:T(8,128)}), f32[32,24,384]{2,1,0:T(8,128)}, u32[]{:S(2)}, u32[]{:S(2)}) async-start(f32[32,24,384]{2,1,0:T(8,128)} %bitcast.52), calls=%async_computation.1 | async-start | bytes 2359296 | tf_op jit(solution)/shard_map/all_to_all | solution.py:612
  40.7 17.9 %collective-permute-start = (f32[4,2,24,384]{3,2,1,0:T(8,128)}, f32[4,2,24,384]{3,2,1,0:T(8,128)}, u32[]{:S(2)}, u32[]{:S(2)}) collective-permute-start(f32[4,2,24,384]{3,2,1,0:T(8,128)} %get-tuple-element.69), channel_id=1, source_target_pairs={{0,8},{8,16},{16,24},{24,0},{1,9},{9,17},{17,25},{25,1},{2,10},{10... | collective-permute-start | bytes 884744 | tf_op jit(solution)/shard_map/ppermute | solution.py:576
  40.9 19.4 %collective-permute-start.1 = (f32[4,2,24,384]{3,2,1,0:T(8,128)}, f32[4,2,24,384]{3,2,1,0:T(8,128)}, u32[]{:S(2)}, u32[]{:S(2)}) collective-permute-start(f32[4,2,24,384]{3,2,1,0:T(8,128)} %get-tuple-element.70), channel_id=1, source_target_pairs={{0,16},{8,24},{16,0},{24,8},{1,17},{9,25},{17,1},{25,9},{2,18},{10... | collective-permute-start | bytes 884744 | tf_op jit(solution)/shard_map/ppermute | solution.py:576
  42.5 22.6 %collective-permute-start.2 = (f32[4,2,24,384]{3,2,1,0:T(8,128)}, f32[4,2,24,384]{3,2,1,0:T(8,128)}, u32[]{:S(2)}, u32[]{:S(2)}) collective-permute-start(f32[4,2,24,384]{3,2,1,0:T(8,128)} %get-tuple-element.71), channel_id=1, source_target_pairs={{0,24},{8,0},{16,8},{24,16},{1,25},{9,1},{17,9},{25,17},{2,26},{10... | collective-permute-start | bytes 884744 | tf_op jit(solution)/shard_map/ppermute | solution.py:576
  85.7 66.7 %all-to-all-start.2 = ((f32[32,24,384]{2,1,0:T(8,128)}), f32[32,24,384]{2,1,0:T(8,128)}, u32[]{:S(2)}, u32[]{:S(2)}) async-start(f32[32,24,384]{2,1,0:T(8,128)} %bitcast.56), calls=%async_computation.2 | async-start | bytes 2359296 | tf_op jit(solution)/shard_map/all_to_all | solution.py:612
  93.6 25.9 %collective-permute-start.3 = (f32[4,2,48,384]{3,2,1,0:T(8,128)}, f32[4,2,48,384]{3,2,1,0:T(8,128)}, u32[]{:S(2)}, u32[]{:S(2)}) collective-permute-start(f32[4,2,48,384]{3,2,1,0:T(8,128)} %get-tuple-element.73), channel_id=1, source_target_pairs={{0,8},{8,16},{16,24},{24,0},{1,9},{9,17},{17,25},{25,1},{2,10},{10... | collective-permute-start | bytes 1769480 | tf_op jit(solution)/shard_map/ppermute | solution.py:576
  93.8 27.2 %collective-permute-start.4 = (f32[4,2,48,384]{3,2,1,0:T(8,128)}, f32[4,2,48,384]{3,2,1,0:T(8,128)}, u32[]{:S(2)}, u32[]{:S(2)}) collective-permute-start(f32[4,2,48,384]{3,2,1,0:T(8,128)} %get-tuple-element.74), channel_id=1, source_target_pairs={{0,16},{8,24},{16,0},{24,8},{1,17},{9,25},{17,1},{25,9},{2,18},{10... | collective-permute-start | bytes 1769480 | tf_op jit(solution)/shard_map/ppermute | solution.py:576
  95.5 36.8 %collective-permute-start.5 = (f32[4,2,48,384]{3,2,1,0:T(8,128)}, f32[4,2,48,384]{3,2,1,0:T(8,128)}, u32[]{:S(2)}, u32[]{:S(2)}) collective-permute-start(f32[4,2,48,384]{3,2,1,0:T(8,128)} %get-tuple-element.75), channel_id=1, source_target_pairs={{0,24},{8,0},{16,8},{24,16},{1,25},{9,1},{17,9},{25,17},{2,26},{10... | collective-permute-start | bytes 1769480 | tf_op jit(solution)/shard_map/ppermute | solution.py:576
  152.4 75.4 %all-to-all-start.3 = ((f32[32,48,384]{2,1,0:T(8,128)}), f32[32,48,384]{2,1,0:T(8,128)}, u32[]{:S(2)}, u32[]{:S(2)}) async-start(f32[32,48,384]{2,1,0:T(8,128)} %bitcast.45), calls=%async_computation.3 | async-start | bytes 4718592 | tf_op jit(solution)/shard_map/all_to_all | solution.py:612
  158.7 34.6 %collective-permute-start.6 = (f32[4,2,48,384]{3,2,1,0:T(8,128)}, f32[4,2,48,384]{3,2,1,0:T(8,128)}, u32[]{:S(2)}, u32[]{:S(2)}) collective-permute-start(f32[4,2,48,384]{3,2,1,0:T(8,128)} %get-tuple-element.77), channel_id=1, source_target_pairs={{0,8},{8,16},{16,24},{24,0},{1,9},{9,17},{17,25},{25,1},{2,10},{10... | collective-permute-start | bytes 1769480 | tf_op jit(solution)/shard_map/ppermute | solution.py:576
  159.0 36.3 %collective-permute-start.7 = (f32[4,2,48,384]{3,2,1,0:T(8,128)}, f32[4,2,48,384]{3,2,1,0:T(8,128)}, u32[]{:S(2)}, u32[]{:S(2)}) collective-permute-start(f32[4,2,48,384]{3,2,1,0:T(8,128)} %get-tuple-element.78), channel_id=1, source_target_pairs={{0,16},{8,24},{16,0},{24,8},{1,17},{9,25},{17,1},{25,9},{2,18},{10... | collective-permute-start | bytes 1769480 | tf_op jit(solution)/shard_map/ppermute | solution.py:576
  160.6 47.1 %collective-permute-start.8 = (f32[4,2,48,384]{3,2,1,0:T(8,128)}, f32[4,2,48,384]{3,2,1,0:T(8,128)}, u32[]{:S(2)}, u32[]{:S(2)}) collective-permute-start(f32[4,2,48,384]{3,2,1,0:T(8,128)} %get-tuple-element.79), channel_id=1, source_target_pairs={{0,24},{8,0},{16,8},{24,16},{1,25},{9,1},{17,9},{25,17},{2,26},{10... | collective-permute-start | bytes 1769480 | tf_op jit(solution)/shard_map/ppermute | solution.py:576
  227.8 10.2 %copy-start.4 = (f32[4,2,48,384]{3,2,1,0:T(8,128)S(1)}, f32[4,2,48,384]{3,2,1,0:T(8,128)}, u32[]{:S(2)}) copy-start(f32[4,2,48,384]{3,2,1,0:T(8,128)} %get-tuple-element.81) | copy-start | bytes 1769476
  227.8 10.5 %copy-start.3 = (f32[4,2,48,384]{3,2,1,0:T(8,128)S(1)}, f32[4,2,48,384]{3,2,1,0:T(8,128)}, u32[]{:S(2)}) copy-start(f32[4,2,48,384]{3,2,1,0:T(8,128)} %get-tuple-element.82) | copy-start | bytes 1769476
  227.9 12.1 %copy-start.2 = (f32[4,2,48,384]{3,2,1,0:T(8,128)S(1)}, f32[4,2,48,384]{3,2,1,0:T(8,128)}, u32[]{:S(2)}) copy-start(f32[4,2,48,384]{3,2,1,0:T(8,128)} %get-tuple-element.83) | copy-start | bytes 1769476
  227.9 79.2 %all-to-all-start.4 = ((f32[32,48,384]{2,1,0:T(8,128)}), f32[32,48,384]{2,1,0:T(8,128)}, u32[]{:S(2)}, u32[]{:S(2)}) async-start(f32[32,48,384]{2,1,0:T(8,128)} %bitcast.46), calls=%async_computation.4 | async-start | bytes 4718592 | tf_op jit(solution)/shard_map/all_to_all | solution.py:612
  238.1 34.6 %collective-permute-start.9 = (f32[4,2,48,384]{3,2,1,0:T(8,128)S(1)}, f32[4,2,48,384]{3,2,1,0:T(8,128)}, u32[]{:S(2)}, u32[]{:S(2)}) collective-permute-start(f32[4,2,48,384]{3,2,1,0:T(8,128)S(1)} %copy-done.4), channel_id=1, source_target_pairs={{0,8},{8,16},{16,24},{24,0},{1,9},{9,17},{17,25},{25,1},{2,10},{10... | collective-permute-start | bytes 1769480 | tf_op jit(solution)/shard_map/ppermute | solution.py:576
  238.3 36.3 %collective-permute-start.10 = (f32[4,2,48,384]{3,2,1,0:T(8,128)S(1)}, f32[4,2,48,384]{3,2,1,0:T(8,128)}, u32[]{:S(2)}, u32[]{:S(2)}) collective-permute-start(f32[4,2,48,384]{3,2,1,0:T(8,128)S(1)} %copy-done.3), channel_id=1, source_target_pairs={{0,16},{8,24},{16,0},{24,8},{1,17},{9,25},{17,1},{25,9},{2,18},{10... | collective-permute-start | bytes 1769480 | tf_op jit(solution)/shard_map/ppermute | solution.py:576
  239.9 46.9 %collective-permute-start.11 = (f32[4,2,48,384]{3,2,1,0:T(8,128)S(1)}, f32[4,2,48,384]{3,2,1,0:T(8,128)}, u32[]{:S(2)}, u32[]{:S(2)}) collective-permute-start(f32[4,2,48,384]{3,2,1,0:T(8,128)S(1)} %copy-done.2), channel_id=1, source_target_pairs={{0,24},{8,0},{16,8},{24,16},{1,25},{9,1},{17,9},{25,17},{2,26},{10... | collective-permute-start | bytes 1769480 | tf_op jit(solution)/shard_map/ppermute | solution.py:576
  307.0 66.0 %all-to-all-start = ((f32[32,48,384]{2,1,0:T(8,128)}), f32[32,48,384]{2,1,0:T(8,128)}, u32[]{:S(2)}, u32[]{:S(2)}) async-start(f32[32,48,384]{2,1,0:T(8,128)} %bitcast.44), calls=%async_computation | async-start | bytes 4718592 | tf_op jit(solution)/shard_map/all_to_all | solution.py:612
